TPU v7x, 512 devices: a whole 4x4x16 slice. The times are simulated.
512 devices in a mesh: box: 128 (over z, y, core), level: 4 (over x).
Axes of the slice: x: 4, y: 4, z: 16, core: 2. Of those that a mesh axis runs over, the one named last changes fastest.
Arguments:
- rhs_field: float32 [4, 2048, 128], P(None, 'box'), may hold values from -6 to 6
- self_coef: float32 [2048, 128], P('box'), may hold values from 2 to 4
- expand: bfloat16 [2048, 256, 128], P('box'), may hold values from -0.5 to 0.5
- near_ops: bfloat16 [26, 128, 128], replicated, may hold values from -0.109375 to 0.109375
- class_ops: bfloat16 [128, 256, 256], P('box', 'level'), may hold values from -0.046875 to 0.046875
- near_src: int32 [2048, 26], P('box'), may hold values from 0 to 47
- send_rows: int32 [128, 128, 2], P('box'), may hold values from 0 to 15
- list_slot: int32 [2048, 64], P('box'), may hold values from 0 to 255
- list_class: int32 [2048, 64], P('box'), may hold values from 0 to 127, all different within a row
Outputs:
- solution: float32 [4, 2048, 128], P(None, 'box')
Inputs may be any that keep to these rules, and one draw needn't show every extreme that they name: `near_src`: the near-field neighbours of a box lie among the boxes of the index of box before it, its own and the one after it, counted in that order. `send_rows`: each entry is a box of the sending index. `list_slot`: entry q * 2 + j names the j-th row sent by index q of box. `list_class`: the classes of one box's list are distinct.
All inputs are finite; a program needn't handle non-finite values.
Results may differ from a plain program's by a relative error of at most 0.004.
Values may be sent and summed in bfloat16 or wider, within the bound.
A program may use at most 64 MiB of HBM per device.

v0:
```python
import math

import jax
import jax.numpy as jnp
from jax import lax
from jax.sharding import PartitionSpec as P


def extended_2(block, sides, width):
    for axis, dim in sides:
        count = lax.axis_size(axis)
        forward = [(i, i + 1) for i in range(count - 1)]
        backward = [(target, source) for source, target in forward]
        low = lax.ppermute(
            lax.slice_in_dim(block, block.shape[dim] - width, None, axis=dim), axis, forward
        )
        high = lax.ppermute(lax.slice_in_dim(block, 0, width, axis=dim), axis, backward)
        block = jnp.concatenate([low, block, high], axis=dim)
    return block


def slot_table(list_slot, list_class, classes):
    labels = jnp.arange(classes, dtype=jnp.int32)
    matches = list_class[:, :, None] == labels[None, None, :]
    return jnp.sum(jnp.where(matches, list_slot[:, :, None] + 1, 0), axis=1) - 1


def apply_classes(totals, operators, offset, table, received):
    count = operators.shape[0]
    picked = lax.dynamic_slice_in_dim(table, offset, count, 1)
    sources = jnp.where(
        (picked >= 0)[:, :, None, None],
        received[jnp.maximum(picked, 0)],
        jnp.zeros((), received.dtype),
    )
    return totals + jnp.einsum(
        "cqp,tcrp->trq", operators, sources, preferred_element_type=jnp.float32
    )


def fold_classes(totals, pieces, offset, table, received):
    count = pieces.shape[0]
    stride = math.gcd(count, 16)

    def step_once(number, current):
        operators = lax.dynamic_slice_in_dim(pieces, number * stride, stride, 0)
        return apply_classes(current, operators, offset + number * stride, table, received)

    return lax.fori_loop(0, count // stride, step_once, totals)


def inner(first, second):
    return jnp.sum(first * second, axis=(1, 2))


def spread(values, field):
    return values[:, None, None] * field


def per_device(
    rhs_field, self_coef, expand, near_ops, class_ops, near_src, send_rows, list_slot, list_class
):
    boxes = expand.shape[0]
    band = class_ops.shape[1]
    classes = class_ops.shape[0] * lax.axis_size("box")
    table = slot_table(list_slot, list_class, classes)
    level_index = lax.axis_index("level")
    cached = lax.all_gather(class_ops, "box", axis=0, tiled=True)

    def apply_matrix(field):
        field_half = field.astype(jnp.bfloat16)
        multipoles = jnp.einsum(
            "tpk,rtk->trp", expand, field_half, preferred_element_type=jnp.float32
        ).astype(jnp.bfloat16)
        outgoing = multipoles[send_rows[0]]
        received = lax.all_to_all(outgoing, "box", split_axis=0, concat_axis=0, tiled=True)
        received = received.reshape((-1,) + received.shape[2:])
        extended = extended_2(field_half, (("box", 1),), boxes)
        neighbours = extended[:, near_src]
        near_part = jnp.einsum(
            "kij,rtkj->rti", near_ops, neighbours, preferred_element_type=jnp.float32
        )
        empty = jnp.zeros((boxes, field.shape[0], band), jnp.float32)
        local_full = fold_classes(empty, cached, 0, table, received)
        local_half = local_full.astype(jnp.bfloat16)
        expand_rows = lax.dynamic_slice_in_dim(expand, level_index * band, band, 1)
        partial_field = jnp.einsum(
            "tqk,trq->rtk", expand_rows, local_half, preferred_element_type=jnp.float32
        )
        far_part = lax.psum(partial_field.astype(jnp.bfloat16), "level").astype(jnp.float32)
        return self_coef[None] * field + near_part + far_part

    def orthogonalize(basis, image):
        stacked = jnp.stack([inner(vector, image) for vector in basis])
        coeffs = lax.psum(stacked, "box")
        for position in range(len(basis)):
            image = image - spread(coeffs[position], basis[position])
        height = jnp.sqrt(lax.psum(inner(image, image), "box"))
        return (coeffs, height, image / height[:, None, None])

    beta = jnp.sqrt(lax.psum(inner(rhs_field, rhs_field), "box"))
    first = rhs_field / beta[:, None, None]
    coeffs_one, h_two_one, second = orthogonalize([first], apply_matrix(first))
    coeffs_two, h_three_two, unused_next = orthogonalize([first, second], apply_matrix(second))
    h_one_one = coeffs_one[0]
    h_one_two = coeffs_two[0]
    h_two_two = coeffs_two[1]
    gram_aa = h_one_one * h_one_one + h_two_one * h_two_one
    gram_ab = h_one_one * h_one_two + h_two_one * h_two_two
    gram_bb = h_one_two * h_one_two + h_two_two * h_two_two + h_three_two * h_three_two
    right_a = beta * h_one_one
    right_b = beta * h_one_two
    determinant = gram_aa * gram_bb - gram_ab * gram_ab
    coef_a = (gram_bb * right_a - gram_ab * right_b) / determinant
    coef_b = (gram_aa * right_b - gram_ab * right_a) / determinant
    return spread(coef_a, first) + spread(coef_b, second)


def solution(mesh):
    return jax.shard_map(
        per_device,
        mesh=mesh,
        in_specs=(
            P(None, "box", None),
            P("box", None),
            P("box", None, None),
            P(),
            P("box", "level", None),
            P("box", None),
            P("box", None, None),
            P("box", None),
            P("box", None),
        ),
        out_specs=P(None, "box", None),
        check_vma=False,
    )
```

profile of v0, /device:TPU:1, one launch (start us, length us, event | category | flops | bytes accessed | tf_op | source)
XLA Modules:
  0.0 1431.7 jit_solution(4672311969668303624)
XLA Ops:
  8.1 254.9 %psum.49 = f32[4]{0:T(128)S(1)} all-reduce(f32[4]{0:T(128)S(1)} %multiply_reduce_fusion.5), channel_id=1, replica_groups=mesh['box'=128,'level'=4] {'box'}, use_global_device_ids=true, to_apply=%region_1.2 | all-reduce | flops 4 | bytes 32 | tf_op jit(solution)/shard_map/psum | solution.py:101
  265.2 1.9 gather_fusion.3
  267.1 12.2 all-to-all-start
  279.3 2.8 collective-permute-start.1
  282.1 2.8 collective-permute-start
  287.6 2.2 gather_fusion.2
  289.8 20.4 %all-to-all-done = bf16[128,2,4,256]{3,2,1,0:T(4,128)(2,1)S(1)} async-done(((bf16[128,2,4,256]{3,2,1,0:T(4,128)(2,1)}), bf16[128,2,4,256]{3,2,1,0:T(4,128)(2,1)S(1)}, u32[]{:S(2)}, u32[]{:S(2)}) %all-to-all-start) | async-done | bytes 524320 | tf_op jit(solution)/shard_map/all_to_all | solution.py:76
  310.2 24.4 %while.28 = (s32[]{:T(128)}, f32[16,4,64]{2,0,1:T(8,128)S(1)}, s32[16,128]{1,0:T(8,128)S(1)}, bf16[256,4,256]{2,1,0:T(4,128)(2,1)S(1)}, bf16[128,64,256]{2,1,0:T...) while((s32[]{:T(128)}, f32[16,4,64]{2,0,1:T(8,128)S(1)}, ...), condition=%wide.region_4.5_spmd.clone, body=%wide.region_3.4_spmd.clone.sunk | while | flops 33826312 | bytes 2142377 | solution.py:49
  314.7 1.5 fusion.43
  320.8 1.5 fusion.43
  323.9 1.5 fusion.43
  327.0 1.5 fusion.43
  334.8 13.1 psum.50
  348.5 251.4 %psum.51 = f32[4]{0:T(128)S(1)} all-reduce(f32[4]{0:T(128)S(1)} %get-tuple-element.259), channel_id=1, replica_groups=mesh['box'=128,'level'=4] {'box'}, use_global_device_ids=true, to_apply=%region_7.8 | all-reduce | flops 4 | bytes 32 | tf_op jit(solution)/shard_map/psum | solution.py:95
  600.1 246.8 %psum.52 = f32[4]{0:T(128)S(1)} all-reduce(f32[4]{0:T(128)S(1)} %multiply_reduce_fusion.3), channel_id=1, replica_groups=mesh['box'=128,'level'=4] {'box'}, use_global_device_ids=true, to_apply=%region_9.10 | all-reduce | flops 4 | bytes 32 | tf_op jit(solution)/shard_map/psum | solution.py:98
  847.4 1.9 gather_fusion.5
  849.3 9.8 all-to-all-start.1
  859.1 2.8 collective-permute-start.3
  861.9 2.8 collective-permute-start.2
  865.6 2.2 gather_fusion.4
  867.8 22.2 %all-to-all-done.1 = bf16[128,2,4,256]{3,2,1,0:T(4,128)(2,1)S(1)} async-done(((bf16[128,2,4,256]{3,2,1,0:T(4,128)(2,1)}), bf16[128,2,4,256]{3,2,1,0:T(4,128)(2,1)S(1)}, u32[]{:S(2)}, u32[]{:S(2)}) %all-to-all-start.1) | async-done | bytes 524320 | tf_op jit(solution)/shard_map/all_to_all | solution.py:76
  889.9 24.4 %while.29 = (s32[]{:T(128)}, f32[16,4,64]{2,0,1:T(8,128)S(1)}, s32[16,128]{1,0:T(8,128)S(1)}, bf16[256,4,256]{2,1,0:T(4,128)(2,1)S(1)}, bf16[128,64,256]{2,1,0:T...) while((s32[]{:T(128)}, f32[16,4,64]{2,0,1:T(8,128)S(1)}, ...), condition=%wide.region_11.12_spmd.clone, body=%wide.region_10.11_spmd.clone.sunk | while | flops 33826312 | bytes 2142377 | solution.py:49
  894.5 1.5 fusion.45
  897.5 1.5 fusion.45
  900.6 1.5 fusion.45
  903.7 1.5 fusion.45
  906.7 1.5 fusion.45
  909.8 1.5 fusion.45
  912.8 1.5 fusion.45
  914.6 10.8 psum.53
  925.9 251.2 %psum.54 = f32[2,4]{1,0:T(2,128)S(1)} all-reduce(f32[2,4]{1,0:T(2,128)S(1)} %pad_maximum_fusion.2), channel_id=1, replica_groups=mesh['box'=128,'level'=4] {'box'}, use_global_device_ids=true, to_apply=%region_15.16 | all-reduce | flops 8 | bytes 64 | tf_op jit(solution)/shard_map/psum | solution.py:95
  1177.3 246.8 %psum.55 = f32[4]{0:T(128)S(1)} all-reduce(f32[4]{0:T(128)S(1)} %multiply_reduce_fusion), channel_id=1, replica_groups=mesh['box'=128,'level'=4] {'box'}, use_global_device_ids=true, to_apply=%region_17.18 | all-reduce | flops 4 | bytes 32 | tf_op jit(solution)/shard_map/psum | solution.py:98
  (153 shorter events, 41.7 us)
Async XLA Ops:
  6.5 258.3 %copy-start = (bf16[16,256,128]{2,1,0:T(8,128)(2,1)S(1)}, bf16[16,256,128]{2,1,0:T(8,128)(2,1)}, u32[]{:S(2)}) copy-start(bf16[16,256,128]{2,1,0:T(8,128)(2,1)} %param.15) | copy-start | bytes 3145732
  6.5 303.6 %all-gather.2.cloned.1.call-start = ((), (), s32[]{:S(2)}) async-start(), calls=%async_computation.2 | async-start | bytes 4227072 | tf_op jit(solution)/shard_map/all_gather | solution.py:68
  267.1 43.1 %all-to-all-start = ((bf16[128,2,4,256]{3,2,1,0:T(4,128)(2,1)}), bf16[128,2,4,256]{3,2,1,0:T(4,128)(2,1)S(1)}, u32[]{:S(2)}, u32[]{:S(2)}) async-start(bf16[128,2,4,256]{3,2,1,0:T(4,128)(2,1)} %bitcast.6), calls=%async_computation | async-start | bytes 1048576 | tf_op jit(solution)/shard_map/all_to_all | solution.py:76
  279.3 8.2 collective-permute-start.1
  282.1 5.4 collective-permute-start
  310.2 37.8 %copy-start.1 = (bf16[26,128,128]{2,1,0:T(8,128)(2,1)S(1)}, bf16[26,128,128]{2,1,0:T(8,128)(2,1)}, u32[]{:S(2)}) copy-start(bf16[26,128,128]{2,1,0:T(8,128)(2,1)} %param.16) | copy-start | bytes 2555908
  310.2 37.8 %copy-start.2 = (f32[4,16,128]{2,1,0:T(8,128)S(1)}, f32[4,16,128]{2,1,0:T(8,128)}, u32[]{:S(2)}) copy-start(f32[4,16,128]{2,1,0:T(8,128)} %param.13) | copy-start | bytes 98308
  310.2 37.8 %copy-start.3 = (f32[16,128]{1,0:T(8,128)S(1)}, f32[16,128]{1,0:T(8,128)}, u32[]{:S(2)}) copy-start(f32[16,128]{1,0:T(8,128)} %param.14) | copy-start | bytes 24580
  849.3 40.6 %all-to-all-start.1 = ((bf16[128,2,4,256]{3,2,1,0:T(4,128)(2,1)}), bf16[128,2,4,256]{3,2,1,0:T(4,128)(2,1)S(1)}, u32[]{:S(2)}, u32[]{:S(2)}) async-start(bf16[128,2,4,256]{3,2,1,0:T(4,128)(2,1)} %bitcast.13), calls=%async_computation.1 | async-start | bytes 1048576 | tf_op jit(solution)/shard_map/all_to_all | solution.py:76
  859.1 5.6 collective-permute-start.3
  861.9 3.6 collective-permute-start.2
Sparse Core Ops, SparseCore 0:
  10.5 147.6 all-gather.1
where the time goes:
time: 1430 us
  blocking collectives  1270 us (89%)
  waiting for transfers between devices  44.1 us (3%)
  starting transfers between devices  33.2 us (2%)
  local copies, waits for them, and re-layouts  29.9 us (2%)
  matrix products  26.6 us (2%)
    psum x2, blocking collectives, orthogonalize(): coeffs = lax.psum(stacked, 'box')  503 us
    psum x2, blocking collectives, orthogonalize(): height = jnp.sqrt(lax.psum(inner(image, image), 'box'))  494 us
    psum x1, blocking collectives, per_device(): beta = jnp.sqrt(lax.psum(inner(rhs_field, rhs_field), 'box'))  255 us
    all_to_all x2, waiting for transfers between devices, apply_matrix(): lax.all_to_all(outgoing, 'box', split_axis=0, concat_axis=0, tiled=True)  42.6 us
  transfers between devices with their start and end apart: 7, of which 3 were waited for; matrix products, arithmetic and copies ran while one was open for 1% of the time, Pallas kernels for 0%

commit v1 on v0

--- a/solution.py
+++ b/solution.py
@@ -90,30 +90,35 @@
         far_part = lax.psum(partial_field.astype(jnp.bfloat16), "level").astype(jnp.float32)
         return self_coef[None] * field + near_part + far_part
 
-    def orthogonalize(basis, image):
-        stacked = jnp.stack([inner(vector, image) for vector in basis])
-        coeffs = lax.psum(stacked, "box")
-        for position in range(len(basis)):
-            image = image - spread(coeffs[position], basis[position])
-        height = jnp.sqrt(lax.psum(inner(image, image), "box"))
-        return (coeffs, height, image / height[:, None, None])
+    def totals(*pairs):
+        stacked = jnp.stack([inner(a, b) for a, b in pairs])
+        return jnp.sum(lax.all_gather(stacked, "box"), axis=0)
 
-    beta = jnp.sqrt(lax.psum(inner(rhs_field, rhs_field), "box"))
-    first = rhs_field / beta[:, None, None]
-    coeffs_one, h_two_one, second = orthogonalize([first], apply_matrix(first))
-    coeffs_two, h_three_two, unused_next = orthogonalize([first, second], apply_matrix(second))
-    h_one_one = coeffs_one[0]
-    h_one_two = coeffs_two[0]
-    h_two_two = coeffs_two[1]
+    first_image = apply_matrix(rhs_field)
+    rr, ra = totals((rhs_field, rhs_field), (rhs_field, first_image))
+    h_one_one = ra / rr
+    second = first_image - spread(h_one_one, rhs_field)
+    second_image = apply_matrix(second)
+    uu, rb, ub, bb = totals(
+        (second, second),
+        (rhs_field, second_image),
+        (second, second_image),
+        (second_image, second_image),
+    )
+    beta = jnp.sqrt(rr)
+    length = jnp.sqrt(uu)
+    h_two_one = length / beta
+    h_one_two = rb / (beta * length)
+    h_two_two = ub / uu
     gram_aa = h_one_one * h_one_one + h_two_one * h_two_one
     gram_ab = h_one_one * h_one_two + h_two_one * h_two_two
-    gram_bb = h_one_two * h_one_two + h_two_two * h_two_two + h_three_two * h_three_two
+    gram_bb = bb / uu
     right_a = beta * h_one_one
     right_b = beta * h_one_two
     determinant = gram_aa * gram_bb - gram_ab * gram_ab
     coef_a = (gram_bb * right_a - gram_ab * right_b) / determinant
     coef_b = (gram_aa * right_b - gram_ab * right_a) / determinant
-    return spread(coef_a, first) + spread(coef_b, second)
+    return spread(coef_a / beta, rhs_field) + spread(coef_b / length, second)
 
 
 def solution(mesh):

time: 1430 us -> 478 us (0.33)
  blocking collectives: 1270 us -> 214 us
  waiting for transfers between devices: 44.1 us -> 142 us
    psum x5 -> x0, blocking collectives: 1250 us -> none  [the longest x2 503 us: orthogonalize(): coeffs = lax.psum(stacked, 'box')]
    all_gather x0 -> x2, blocking collectives: none -> 190 us  [totals(): return jnp.sum(lax.all_gather(stacked, 'box'), axis=0)]
    all_gather x1, waiting for transfers between devices: 0.01 us -> 96.6 us  [per_device(): cached = lax.all_gather(class_ops, 'box', axis=0, tiled=True)]
  transfers between devices with their start and end apart: 7 -> 7, of which waited for: 3 -> 4; matrix products, arithmetic and copies ran while one was open for 1% -> 2% of each run, Pallas kernels for 0% -> 0%
where the time goes in v1:
time: 478 us; the launch traced here: 477 us
  blocking collectives  214 us (45%)
  waiting for transfers between devices  142 us (30%)
  starting transfers between devices  42.2 us (9%)
  local copies, waits for them, and re-layouts  30.7 us (6%)
  matrix products  26.8 us (6%)
  between operations  13.6 us (3%)
  other arithmetic  6.97 us (1%)
    all_gather x2, blocking collectives, totals(): return jnp.sum(lax.all_gather(stacked, 'box'), axis=0)  190 us
    all_gather x1, waiting for transfers between devices, per_device(): cached = lax.all_gather(class_ops, 'box', axis=0, tiled=True)  96.6 us
    all_to_all x2, waiting for transfers between devices, apply_matrix(): lax.all_to_all(outgoing, 'box', split_axis=0, concat_axis=0, tiled=True)  44.1 us
    all_to_all x2, starting transfers between devices, apply_matrix(): lax.all_to_all(outgoing, 'box', split_axis=0, concat_axis=0, tiled=True)  30.9 us
    dot_general x16, matrix products, apply_classes(): jnp.einsum('cqp,tcrp->trq', operators, sources, preferred_element_type=jn...  24.6 us
    psum x2, blocking collectives, apply_matrix(): lax.psum(partial_field.astype(jnp.bfloat16), 'level').astype(jnp.float32)  23.9 us
    gather x16, local copies, waits for them, and re-layouts, apply_classes(): received[jnp.maximum(picked, 0)]  18.5 us
  transfers between devices with their start and end apart: 7, of which 4 were waited for; matrix products, arithmetic and copies ran while one was open for 2% of the time, Pallas kernels for 0%

profile of v1, /device:TPU:1, one launch (start us, length us, event | category | flops | bytes accessed | tf_op | source)
XLA Modules:
  0.0 477.1 jit_solution(12812204908708037069)
XLA Ops:
  9.4 1.9 gather_fusion.3
  11.3 20.6 %all-to-all-start = ((bf16[128,2,4,256]{3,2,1,0:T(4,128)(2,1)}), bf16[128,2,4,256]{3,2,1,0:T(4,128)(2,1)S(1)}, u32[]{:S(2)}, u32[]{:S(2)}) async-start(bf16[128,2,4,256]{3,2,1,0:T(4,128)(2,1)} %bitcast.6), calls=%async_computation | async-start | bytes 1048576 | tf_op jit(solution)/shard_map/all_to_all | solution.py:76
  31.9 2.8 collective-permute-start.1
  34.7 2.8 collective-permute-start
  40.1 2.2 gather_fusion.2
  42.3 21.9 %all-to-all-done = bf16[128,2,4,256]{3,2,1,0:T(4,128)(2,1)S(1)} async-done(((bf16[128,2,4,256]{3,2,1,0:T(4,128)(2,1)}), bf16[128,2,4,256]{3,2,1,0:T(4,128)(2,1)S(1)}, u32[]{:S(2)}, u32[]{:S(2)}) %all-to-all-start) | async-done | bytes 524320 | tf_op jit(solution)/shard_map/all_to_all | solution.py:76
  64.2 96.6 %all-gather.6.cloned.1.call-done = bf16[128,64,256]{2,1,0:T(8,128)(2,1)} async-done(((bf16[1,64,256]{2,1,0:T(8,128)(2,1)}), bf16[128,64,256]{2,1,0:T(8,128)(2,1)}) %all-gather.6.cloned.1.call-update) | async-done | bytes 4194320 | tf_op jit(solution)/shard_map/all_gather | solution.py:68
  160.8 24.6 %while.28 = (s32[]{:T(128)}, f32[16,4,64]{2,0,1:T(8,128)S(1)}, s32[16,128]{1,0:T(8,128)S(1)}, bf16[256,4,256]{2,1,0:T(4,128)(2,1)S(1)}, bf16[128,64,256]{2,1,0:T...) while((s32[]{:T(128)}, f32[16,4,64]{2,0,1:T(8,128)S(1)}, ...), condition=%wide.region_2.3_spmd.clone, body=%wide.region_1.2_spmd.clone.sunk | while | flops 33826312 | bytes 2142377 | solution.py:49
  162.3 1.5 fusion.51
  165.4 1.5 fusion.51
  168.5 1.5 fusion.51
  171.5 1.5 fusion.51
  174.6 1.5 fusion.51
  177.7 1.5 fusion.51
  180.8 1.5 fusion.51
  183.8 1.5 fusion.51
  185.6 13.1 %psum.14 = bf16[4,16,128]{2,1,0:T(8,128)(2,1)S(1)} all-reduce(bf16[4,16,128]{2,1,0:T(8,128)(2,1)S(1)} %bitcast.147), channel_id=1, replica_groups=mesh['box'=128,'level'=4] {'level'}, use_global_device_ids=true, to_apply=%region_3.4 | all-reduce | flops 8192 | bytes 32768 | tf_op jit(solution)/shard_map/psum | solution.py:90
  199.2 84.8 %all-gather.2 = f32[128,2,4]{2,1,0:T(2,128)S(1)} all-gather(f32[1,2,4]{2,1,0:T(2,128)S(1)} %maximum_bitcast_fusion.1), channel_id=2, replica_groups=mesh['box'=128,'level'=4] {'box'}, dimensions={0}, use_global_device_ids=true | all-gather | bytes 4128 | tf_op jit(solution)/shard_map/all_gather | solution.py:95
  284.6 1.9 gather_fusion.5
  286.6 10.3 %all-to-all-start.1 = ((bf16[128,2,4,256]{3,2,1,0:T(4,128)(2,1)}), bf16[128,2,4,256]{3,2,1,0:T(4,128)(2,1)S(1)}, u32[]{:S(2)}, u32[]{:S(2)}) async-start(bf16[128,2,4,256]{3,2,1,0:T(4,128)(2,1)} %bitcast.18), calls=%async_computation.1 | async-start | bytes 1048576 | tf_op jit(solution)/shard_map/all_to_all | solution.py:76
  296.9 2.8 collective-permute-start.3
  299.7 2.9 collective-permute-start.2
  303.4 2.2 gather_fusion.4
  305.6 22.2 %all-to-all-done.1 = bf16[128,2,4,256]{3,2,1,0:T(4,128)(2,1)S(1)} async-done(((bf16[128,2,4,256]{3,2,1,0:T(4,128)(2,1)}), bf16[128,2,4,256]{3,2,1,0:T(4,128)(2,1)S(1)}, u32[]{:S(2)}, u32[]{:S(2)}) %all-to-all-start.1) | async-done | bytes 524320 | tf_op jit(solution)/shard_map/all_to_all | solution.py:76
  327.7 24.5 %while.29 = (s32[]{:T(128)}, f32[16,4,64]{2,0,1:T(8,128)S(1)}, s32[16,128]{1,0:T(8,128)S(1)}, bf16[256,4,256]{2,1,0:T(4,128)(2,1)S(1)}, bf16[128,64,256]{2,1,0:T...) while((s32[]{:T(128)}, f32[16,4,64]{2,0,1:T(8,128)S(1)}, ...), condition=%wide.region_9.10_spmd.clone, body=%wide.region_8.9_spmd.clone.sunk | while | flops 33826312 | bytes 2142377 | solution.py:49
  329.2 1.5 fusion.53
  332.3 1.5 fusion.53
  338.4 1.5 fusion.53
  344.5 1.5 fusion.53
  350.7 1.5 fusion.53
  352.4 10.8 %psum.15 = bf16[4,16,128]{2,1,0:T(8,128)(2,1)S(1)} all-reduce(bf16[4,16,128]{2,1,0:T(8,128)(2,1)S(1)} %bitcast.148), channel_id=1, replica_groups=mesh['box'=128,'level'=4] {'level'}, use_global_device_ids=true, to_apply=%region_10.11 | all-reduce | flops 8192 | bytes 32768 | tf_op jit(solution)/shard_map/psum | solution.py:90
  363.8 105.6 %all-gather.3 = f32[128,4,4]{2,1,0:T(4,128)S(1)} all-gather(f32[1,4,4]{2,1,0:T(4,128)S(1)} %maximum_bitcast_fusion), channel_id=3, replica_groups=mesh['box'=128,'level'=4] {'box'}, dimensions={0}, use_global_device_ids=true | all-gather | bytes 8256 | tf_op jit(solution)/shard_map/all_gather | solution.py:95
  (148 shorter events, 37.5 us)
Async XLA Ops:
  6.5 2.5 copy-start
  6.5 154.3 %all-gather.6.cloned.1.call-start = ((), (), s32[]{:S(2)}) async-start(), calls=%async_computation.2 | async-start | bytes 4227072 | tf_op jit(solution)/shard_map/all_gather | solution.py:68
  11.3 52.9 %all-to-all-start = ((bf16[128,2,4,256]{3,2,1,0:T(4,128)(2,1)}), bf16[128,2,4,256]{3,2,1,0:T(4,128)(2,1)S(1)}, u32[]{:S(2)}, u32[]{:S(2)}) async-start(bf16[128,2,4,256]{3,2,1,0:T(4,128)(2,1)} %bitcast.6), calls=%async_computation | async-start | bytes 1048576 | tf_op jit(solution)/shard_map/all_to_all | solution.py:76
  31.9 8.2 %collective-permute-start.1 = (bf16[4,16,128]{2,0,1:T(4,128)(2,1)S(1)}, bf16[4,16,128]{2,0,1:T(4,128)(2,1)S(1)}, u32[]{:S(2)}, u32[]{:S(2)}) collective-permute-start(bf16[4,16,128]{2,0,1:T(4,128)(2,1)S(1)} %copy.87), channel_id=1, source_target_pairs={{4,0},{8,4},{12,8},{16,12},{20,16},{24,20},{28,24},{32,28},{36,32}... | collective-permute-start | bytes 49160 | tf_op jit(solution)/shard_map/ppermute | solution.py:17
  34.7 5.4 %collective-permute-start = (bf16[4,16,128]{2,0,1:T(4,128)(2,1)S(1)}, bf16[4,16,128]{2,0,1:T(4,128)(2,1)S(1)}, u32[]{:S(2)}, u32[]{:S(2)}) collective-permute-start(bf16[4,16,128]{2,0,1:T(4,128)(2,1)S(1)} %copy.87), channel_id=1, source_target_pairs={{0,4},{4,8},{8,12},{12,16},{16,20},{20,24},{24,28},{28,32},{32,36}... | collective-permute-start | bytes 49160 | tf_op jit(solution)/shard_map/ppermute | solution.py:14
  160.8 37.9 %copy-start.1 = (bf16[26,128,128]{2,1,0:T(8,128)(2,1)S(1)}, bf16[26,128,128]{2,1,0:T(8,128)(2,1)}, u32[]{:S(2)}) copy-start(bf16[26,128,128]{2,1,0:T(8,128)(2,1)} %param.16) | copy-start | bytes 2555908
  160.8 37.9 %copy-start.2 = (f32[4,16,128]{2,1,0:T(8,128)S(1)}, f32[4,16,128]{2,1,0:T(8,128)}, u32[]{:S(2)}) copy-start(f32[4,16,128]{2,1,0:T(8,128)} %param.13) | copy-start | bytes 98308
  160.8 37.9 %copy-start.3 = (f32[16,128]{1,0:T(8,128)S(1)}, f32[16,128]{1,0:T(8,128)}, u32[]{:S(2)}) copy-start(f32[16,128]{1,0:T(8,128)} %param.14) | copy-start | bytes 24580
  286.6 41.2 %all-to-all-start.1 = ((bf16[128,2,4,256]{3,2,1,0:T(4,128)(2,1)}), bf16[128,2,4,256]{3,2,1,0:T(4,128)(2,1)S(1)}, u32[]{:S(2)}, u32[]{:S(2)}) async-start(bf16[128,2,4,256]{3,2,1,0:T(4,128)(2,1)} %bitcast.18), calls=%async_computation.1 | async-start | bytes 1048576 | tf_op jit(solution)/shard_map/all_to_all | solution.py:76
  296.9 5.8 %collective-permute-start.3 = (bf16[4,16,128]{2,1,0:T(8,128)(2,1)S(1)}, bf16[4,16,128]{2,1,0:T(8,128)(2,1)S(1)}, u32[]{:S(2)}, u32[]{:S(2)}) collective-permute-start(bf16[4,16,128]{2,1,0:T(8,128)(2,1)S(1)} %get-tuple-element.261), channel_id=1, source_target_pairs={{4,0},{8,4},{12,8},{16,12},{20,16},{24,20},{28,24},{32,28},{36,32}... | collective-permute-start | bytes 49160 | tf_op jit(solution)/shard_map/ppermute | solution.py:17
  299.7 3.6 collective-permute-start.2
Sparse Core Ops, SparseCore 0:
  10.5 150.2 all-gather.5

commit v2 on v0

v2 whole, which is shorter than its diff:
```python
import jax
import jax.numpy as jnp
from jax import lax
from jax.experimental import pallas as pl
from jax.experimental.pallas import tpu as pltpu
from jax.sharding import PartitionSpec as P

NZ, NY, NC, NX = 16, 4, 2, 4
NYC = NY * NC
SHIFT = 3.0
F32, BF16 = jnp.float32, jnp.bfloat16


def dot(a, b):
    return jnp.dot(a, b, preferred_element_type=F32)


def dot_nt(a, b):
    return lax.dot_general(a, b, (((1,), (1,)), ((), ())), preferred_element_type=F32)


def iota(shape, dim):
    return lax.broadcasted_iota(jnp.int32, shape, dim)


def body(
    rhs_ref, self_ref, expand_hbm, near_hbm, cls_ref, oh_ref, nearoh_ref, sendoh_ref,
    out_ref,
    efull, nops, tout, tin, wbuf, hbuf, obuf, zbuf, pbuf, rbuf, r2, g2, nbuf, xbuf,
    rz_out, rz, ry_out, ry,
    load_sem, t_send, t_recv, ring_send, ring_recv, y_send, y_recv, sib_send, sib_recv,
    h_send, h_recv, z_send, z_recv, p_send, p_recv, x_send, x_recv,
    rz_send, rz_recv, ry_send, ry_recv,
):
    me = lax.axis_index("box")
    x = lax.axis_index("level")
    z = me // NYC
    yc = me % NYC
    y = yc // NC
    core = yc % NC
    sends = []

    def start(src, dst, ssem, rsem, box, level):
        copy = pltpu.make_async_remote_copy(
            src_ref=src, dst_ref=dst, send_sem=ssem, recv_sem=rsem,
            device_id=(box, level), device_id_type=pl.DeviceIdType.MESH,
        )
        copy.start()
        sends.append(copy)

    def arrived(dst, rsem):
        pltpu.make_async_remote_copy(
            src_ref=dst, dst_ref=dst, send_sem=rsem, recv_sem=rsem,
            device_id=(me, x), device_id_type=pl.DeviceIdType.MESH,
        ).wait_recv()

    load_e = pltpu.make_async_copy(expand_hbm, efull, load_sem.at[0])
    load_n = pltpu.make_async_copy(near_hbm, nops, load_sem.at[1])
    load_e.start()
    load_n.start()

    def z_peer(d):
        return ((z + d) % NZ) * NYC + yc

    def p_peer(d):
        return z * NYC + (yc + d) % NYC

    def x_peer(d):
        return (x + d) % NX

    has_low = me > 0
    has_high = me < NZ * NYC - 1

    barrier = pltpu.get_barrier_semaphore()

    def greet(box, level):
        pl.semaphore_signal(
            barrier, inc=1, device_id=(box, level), device_id_type=pl.DeviceIdType.MESH
        )

    for d in range(1, NZ):
        greet(z_peer(d), x)
    for d in range(1, NYC):
        greet(p_peer(d), x)
    for d in range(1, NX):
        greet(me, x_peer(d))

    @pl.when(has_low)
    def _():
        greet(me - 1, x)

    @pl.when(has_high)
    def _():
        greet(me + 1, x)

    cls = cls_ref[...]
    eye2 = jnp.where(iota((64, 128), 0) == iota((64, 128), 1) % 64, 1.0, 0.0).astype(BF16)
    turned = lax.dot_general(
        cls, eye2, (((0,), (0,)), ((), ())), preferred_element_type=F32
    ).astype(BF16)
    tout[...] = turned.reshape(NX, 64, 128)

    pl.semaphore_wait(
        barrier,
        (NZ - 1) + (NYC - 1) + (NX - 1)
        + has_low.astype(jnp.int32) + has_high.astype(jnp.int32),
    )

    for d in range(1, NX):
        start(tout.at[x_peer(d)], tin.at[x], t_send.at[d], t_recv.at[x], me, x_peer(d))
    tin[x] = tout[x]

    lane128 = iota((16, 128), 1)
    low16 = lane128 < 64
    row_t = iota((16, 128), 0)
    rows64 = iota((64, 256), 0) % 16

    def halo_sends(it, v):
        half = v.astype(BF16)
        for r in range(4):
            hbuf[it, 1, :, r * 128:(r + 1) * 128] = half[r * 16:(r + 1) * 16]

        low = pltpu.make_async_remote_copy(
            src_ref=hbuf.at[it, 1], dst_ref=hbuf.at[it, 2],
            send_sem=h_send.at[it, 0], recv_sem=h_recv.at[it, 1],
            device_id=(me - 1, x), device_id_type=pl.DeviceIdType.MESH,
        )
        high = pltpu.make_async_remote_copy(
            src_ref=hbuf.at[it, 1], dst_ref=hbuf.at[it, 0],
            send_sem=h_send.at[it, 1], recv_sem=h_recv.at[it, 0],
            device_id=(me + 1, x), device_id_type=pl.DeviceIdType.MESH,
        )

        @pl.when(has_low)
        def _():
            low.start()

        @pl.when(has_high)
        def _():
            high.start()

        @pl.when(jnp.logical_not(has_low))
        def _():
            hbuf[it, 0] = jnp.zeros((16, 512), BF16)

        @pl.when(jnp.logical_not(has_high))
        def _():
            hbuf[it, 2] = jnp.zeros((16, 512), BF16)

        return half, low, high

    def multipole_sends(it, half):
        band = efull[:, pl.ds(pl.multiple_of(x * 64, 64), 64), :].reshape(1024, 128)
        full = dot_nt(half, band)
        doubled = []
        for r in range(4):
            total = jnp.zeros((16, 128), F32)
            for j in range(8):
                piece = full[r * 16:(r + 1) * 16, j * 128:(j + 1) * 128]
                total = total + jnp.where(
                    row_t == 2 * j + jnp.where(low16, 0, 1), piece, 0.0
                )
            doubled.append(total + pltpu.roll(total, 64, 1))
        rows = jnp.concatenate(
            [
                jnp.where(low16, doubled[0], doubled[1]),
                jnp.where(low16, doubled[2], doubled[3]),
            ],
            axis=1,
        ).astype(BF16)
        obuf[it] = dot(sendoh_ref[...], rows).astype(BF16).reshape(NZ, 16, 256)
        for d in (8, 7, 9, 6, 10, 5, 11, 4, 12, 3, 13, 2, 14, 1, 15):
            to = (z + d) % NZ
            start(obuf.at[it, to], zbuf.at[it, z], z_send.at[it, d], z_recv.at[it, z],
                  to * NYC + yc, x)
        zbuf[it, z] = obuf[it, z]

    def resort_sends(it):
        for d in range(1, NZ):
            src = (z + d) % NZ
            arrived(zbuf.at[it, src], z_recv.at[it, src])
        row = iota((256, 256), 0)
        want = ((row // 2) % 16) * 16 + (row // 32) * 2 + row % 2
        order = jnp.where(want == iota((256, 256), 1), 1.0, 0.0).astype(BF16)
        pbuf[it] = dot(order, zbuf[it].reshape(256, 256)).astype(BF16).reshape(8, 32, 256)
        for d in range(1, NYC):
            to = (yc + d) % NYC
            start(pbuf.at[it, to], rbuf.at[it, yc], p_send.at[it, d], p_recv.at[it, yc],
                  z * NYC + to, x)
        rbuf[it, yc] = pbuf[it, yc]

    def near_field(it, low, high):
        @pl.when(has_low)
        def _():
            high.wait_recv()

        @pl.when(has_high)
        def _():
            low.wait_recv()

        nbuf[...] = dot(nearoh_ref[...], hbuf[it].reshape(48, 512)).astype(BF16)

        def one(c, acc):
            rows = nbuf[pl.ds(pl.multiple_of(c * 16, 16), 16), :]
            lhs = jnp.concatenate([rows[:, r * 128:(r + 1) * 128] for r in range(4)], axis=0)
            return acc + dot_nt(lhs, nops[c])

        return lax.fori_loop(0, 26, one, jnp.zeros((64, 128), F32))

    def pick_sources(it):
        for d in range(1, NYC):
            src = (yc + d) % NYC
            arrived(rbuf.at[it, src], p_recv.at[it, src])
        low = iota((256, 128), 1) < 64
        received = rbuf[it].reshape(256, 256)
        for h in range(2):
            a = received[:, h * 128:(h + 1) * 128].astype(F32)
            b = pltpu.roll(a, 64, 1)
            for r, first, second in ((2 * h, a, b), (2 * h + 1, b, a)):
                lanes = slice(r * 128, (r + 1) * 128)
                r2[0:256, lanes] = jnp.where(low, first, 0.0).astype(BF16)
                r2[256:512, lanes] = jnp.where(low, 0.0, second).astype(BF16)

        def one(i, carry):
            at = pl.ds(pl.multiple_of(i * 128, 128), 128)
            g2[at, :] = dot(oh_ref[at, :], r2[...]).astype(BF16)
            return carry

        lax.fori_loop(0, 8, one, 0)

    def local_far_sends(it):
        def one(i, acc):
            rows = g2[pl.ds(pl.multiple_of(i * 32, 32), 32), :]
            lhs = jnp.concatenate(
                [
                    jnp.concatenate(
                        [rows[0:16, r * 128:(r + 1) * 128], rows[16:32, r * 128:(r + 1) * 128]],
                        axis=1,
                    )
                    for r in range(4)
                ],
                axis=0,
            )
            ops = wbuf[pl.ds(i * 4, 4)].reshape(256, 256)
            return acc + dot(lhs, ops)

        local = lax.fori_loop(0, 32, one, jnp.zeros((64, 256), F32))

        def far_one(t, acc):
            return acc + dot(jnp.where(rows64 == t, local, 0.0).astype(BF16), efull[t])

        far = lax.fori_loop(0, 16, far_one, jnp.zeros((64, 128), F32))
        xbuf[it, x] = far.astype(BF16)
        for d in range(1, NX):
            start(xbuf.at[it, x], xbuf.at[it, x], x_send.at[it, d], x_recv.at[it, x],
                  me, x_peer(d))

    def far_sum(it):
        for d in range(1, NX):
            arrived(xbuf.at[it, x_peer(d)], x_recv.at[it, x_peer(d)])
        total = xbuf[it, 0].astype(F32)
        for k in range(1, NX):
            total = total + xbuf[it, k].astype(F32)
        return total

    lane1 = iota((1, 128), 1)

    def packed(pairs):
        row = jnp.zeros((1, 128), F32)
        for q, (a, b) in enumerate(pairs):
            product = a * b
            for r in range(4):
                value = jnp.sum(
                    jnp.sum(product[r * 16:(r + 1) * 16], axis=0, keepdims=True),
                    axis=1, keepdims=True,
                )
                row = row + jnp.where(lane1 == q * 4 + r, value, 0.0)
        return row

    def reduce_z(it, row):
        rz_out[it] = row
        for d in range(1, NZ):
            start(rz_out.at[it], rz.at[it, z], rz_send.at[it, d], rz_recv.at[it, z],
                  z_peer(d), x)
        rz[it, z] = row

    def reduce_p(it):
        for d in range(1, NZ):
            src = (z + d) % NZ
            arrived(rz.at[it, src], rz_recv.at[it, src])
        row = jnp.sum(rz[it], axis=0)
        ry_out[it] = row
        for d in range(1, NYC):
            start(ry_out.at[it], ry.at[it, yc], ry_send.at[it, d], ry_recv.at[it, yc],
                  p_peer(d), x)
        ry[it, yc] = row

    def reduced(it):
        for d in range(1, NYC):
            src = (yc + d) % NYC
            arrived(ry.at[it, src], ry_recv.at[it, src])
        return jnp.sum(ry[it], axis=0)

    def spread(row):
        return jnp.concatenate(
            [
                jnp.broadcast_to(
                    jnp.sum(jnp.where(lane1 == r, row, 0.0), axis=1, keepdims=True), (16, 128)
                )
                for r in range(4)
            ],
            axis=0,
        )

    v = rhs_ref[...].reshape(64, 128)
    diag = jnp.concatenate([self_ref[...]] * 4, axis=0)
    half, low_copy, high_copy = halo_sends(0, v)
    load_e.wait()
    multipole_sends(0, half)

    for d in range(1, NX):
        arrived(tin.at[x_peer(d)], t_recv.at[x_peer(d)])
    low_t = iota((64, 128), 1) < 64
    pairs = [
        jnp.where(low_t, tin[2 * h].astype(F32), tin[2 * h + 1].astype(F32)) for h in range(2)
    ]
    wbuf[me] = jnp.concatenate(pairs, axis=1).astype(BF16)

    def cls_at(m, y_rel):
        return wbuf.at[((z - m + NZ) % NZ) * NYC + ((y + y_rel) % NY) * NC + core]

    def ring(m_at, step, right):
        ref = cls_at(m_at, 0)
        way = 0 if right else 1
        start(ref, ref, ring_send.at[way, step], ring_recv.at[way, step],
              z_peer(1 if right else NZ - 1), x)

    def y_out(m):
        ref = cls_at(m, 0)
        up = z * NYC + ((y + 1) % NY) * NC + core
        down = z * NYC + ((y + 3) % NY) * NC + core
        start(ref, ref, y_send.at[0, m], y_recv.at[0, m], up, x)
        start(ref, ref, y_send.at[1, m], y_recv.at[1, m], down, x)

    def sibling(m, y_rel):
        ref = cls_at(m, y_rel)
        start(ref, ref, sib_send.at[y_rel, m], sib_recv, z * NYC + y * NC + 1 - core, x)

    def y_in(m):
        arrived(cls_at(m, 3), y_recv.at[0, m])
        arrived(cls_at(m, 1), y_recv.at[1, m])
        if m % 2 == 0:
            ref = cls_at(m, 3)
            to = z * NYC + ((y + 1) % NY) * NC + core
        else:
            ref = cls_at(m, 1)
            to = z * NYC + ((y + 3) % NY) * NC + core
        start(ref, ref, y_send.at[2, m], y_recv.at[2, m], to, x)
        sibling(m, 3)
        sibling(m, 1)

    def y_far_in(m):
        arrived(cls_at(m, 2), y_recv.at[2, m])
        sibling(m, 2)

    def step_set(k):
        if k == 0:
            return [0]
        if k == 8:
            return [8]
        return [k, NZ - k]

    ring(0, 1, True)
    ring(0, 1, False)
    y_out(0)
    sibling(0, 0)

    load_n.wait()
    near_one = near_field(0, low_copy, high_copy)

    for k in range(1, 9):
        arrived(cls_at(k, 0), ring_recv.at[0, k])
        if k < 8:
            ring(k, k + 1, True)
            arrived(cls_at(NZ - k, 0), ring_recv.at[1, k])
            if k < 7:
                ring(NZ - k, k + 1, False)
        for m in step_set(k):
            y_out(m)
            sibling(m, 0)
        for m in step_set(k - 1):
            y_in(m)
        if k >= 2:
            for m in step_set(k - 2):
                y_far_in(m)
        if k == 3:
            resort_sends(0)
        if k == 6:
            pick_sources(0)
    for m in step_set(8):
        y_in(m)
    for k in (7, 8):
        for m in step_set(k):
            y_far_in(m)
    other = wbuf.at[pl.ds(0, 64)]
    arrived(other, sib_recv)

    local_far_sends(0)
    base = diag * v + near_one
    image = base + far_sum(0)

    shifted = image - SHIFT * v
    half, low_two, high_two = halo_sends(1, shifted)
    multipole_sends(1, half)
    reduce_z(0, packed([(v, v), (v, image)]))
    near_two = near_field(1, low_two, high_two)
    resort_sends(1)
    reduce_p(0)
    pick_sources(1)
    local_far_sends(1)

    first_sums = reduced(0)
    rr = first_sums
    ra = pltpu.roll(first_sums, 124, 1)
    h11 = ra / rr
    slope = spread(h11)
    u = image - slope * v
    base = diag * shifted + near_two - (slope - SHIFT) * image
    b = base + far_sum(1)
    reduce_z(1, packed([(u, u), (v, b), (u, b), (b, b)]))
    reduce_p(1)
    second_sums = reduced(1)
    uu = second_sums
    rb = pltpu.roll(second_sums, 124, 1)
    ub = pltpu.roll(second_sums, 120, 1)
    bb = pltpu.roll(second_sums, 116, 1)
    beta = jnp.sqrt(rr)
    length = jnp.sqrt(uu)
    h21 = length / beta
    h12 = rb / (beta * length)
    h22 = ub / uu
    gram_aa = h11 * h11 + h21 * h21
    gram_ab = h11 * h12 + h21 * h22
    gram_bb = bb / uu
    right_a = beta * h11
    right_b = beta * h12
    det = gram_aa * gram_bb - gram_ab * gram_ab
    coef_a = (gram_bb * right_a - gram_ab * right_b) / det / beta
    coef_b = (gram_aa * right_b - gram_ab * right_a) / det / length
    out_ref[...] = (spread(coef_a) * v + spread(coef_b) * u).reshape(4, 16, 128)

    for copy in sends:
        copy.wait_send()
    for low, high in ((low_copy, high_copy), (low_two, high_two)):
        @pl.when(has_low)
        def _():
            low.wait_send()

        @pl.when(has_high)
        def _():
            high.wait_send()


def per_device(
    rhs_field, self_coef, expand, near_ops, class_ops, near_src, send_rows, list_slot, list_class
):
    slot = ((list_slot // 2) % 8) * 32 + (list_slot // 16) * 2 + list_slot % 2
    labels = jnp.arange(128, dtype=jnp.int32)
    matches = list_class[:, None, :] == labels[None, :, None]
    table = jnp.sum(jnp.where(matches, slot[:, None, :] + 1, 0), axis=2) - 1
    table = table.T.reshape(64, 2, 16).transpose(0, 2, 1).reshape(1024, 2, 1)
    hot = (table == jnp.arange(256, dtype=jnp.int32)).astype(BF16).reshape(1024, 512)
    near_hot = (
        near_src.T.reshape(416, 1) == jnp.arange(48, dtype=jnp.int32)
    ).astype(BF16)
    send_hot = (
        send_rows[0].reshape(256, 1) == jnp.arange(16, dtype=jnp.int32)
    ).astype(BF16)

    vmem = pl.BlockSpec(memory_space=pltpu.VMEM)
    hbm = pl.BlockSpec(memory_space=pl.ANY)
    dma = pltpu.SemaphoreType.DMA
    return pl.pallas_call(
        body,
        out_shape=jax.ShapeDtypeStruct((4, 16, 128), F32),
        in_specs=[vmem, vmem, hbm, hbm, vmem, vmem, vmem, vmem],
        out_specs=vmem,
        scratch_shapes=[
            pltpu.VMEM((16, 256, 128), BF16),
            pltpu.VMEM((26, 128, 128), BF16),
            pltpu.VMEM((NX, 64, 128), BF16),
            pltpu.VMEM((NX, 64, 128), BF16),
            pltpu.VMEM((128, 64, 256), BF16),
            pltpu.VMEM((2, 3, 16, 512), BF16),
            pltpu.VMEM((2, NZ, 16, 256), BF16),
            pltpu.VMEM((2, NZ, 16, 256), BF16),
            pltpu.VMEM((2, NYC, 32, 256), BF16),
            pltpu.VMEM((2, NYC, 32, 256), BF16),
            pltpu.VMEM((512, 512), BF16),
            pltpu.VMEM((1024, 512), BF16),
            pltpu.VMEM((416, 512), BF16),
            pltpu.VMEM((2, NX, 64, 128), BF16),
            pltpu.VMEM((2, 1, 128), F32),
            pltpu.VMEM((2, NZ, 1, 128), F32),
            pltpu.VMEM((2, 1, 128), F32),
            pltpu.VMEM((2, NYC, 1, 128), F32),
            dma((2,)),
            dma((NX,)), dma((NX,)),
            dma((2, 9)), dma((2, 9)),
            dma((3, NZ)), dma((3, NZ)),
            dma((NY, NZ)), dma,
            dma((2, 2)), dma((2, 2)),
            dma((2, NZ)), dma((2, NZ)),
            dma((2, NYC)), dma((2, NYC)),
            dma((2, NX)), dma((2, NX)),
            dma((2, NZ)), dma((2, NZ)),
            dma((2, NYC)), dma((2, NYC)),
        ],
        compiler_params=pltpu.CompilerParams(
            collective_id=0, has_side_effects=True, vmem_limit_bytes=40 * 1024 * 1024
        ),
        cost_estimate=pl.CostEstimate(
            flops=4_000_000_000, bytes_accessed=4_000_000, transcendentals=0
        ),
    )(
        rhs_field, self_coef, expand, near_ops, class_ops[0], hot, near_hot, send_hot
    )


def solution(mesh):
    return jax.shard_map(
        per_device,
        mesh=mesh,
        in_specs=(
            P(None, "box", None),
            P("box", None),
            P("box", None, None),
            P(),
            P("box", "level", None),
            P("box", None),
            P("box", None, None),
            P("box", None),
            P("box", None),
        ),
        out_specs=P(None, "box", None),
        check_vma=False,
    )
```

time: 1430 us -> 116 us (0.08)
  blocking collectives: 1270 us -> 0 us
  Pallas kernels: 0 us -> 108 us
  waiting for transfers between devices: 44.1 us -> 0 us
  starting transfers between devices: 33.2 us -> 0 us
  matrix products: 26.6 us -> 0 us
  local copies, waits for them, and re-layouts: 29.9 us -> 4.74 us
    psum x7 -> x0, blocking collectives: 1270 us -> none  [the longest x2 503 us: orthogonalize(): coeffs = lax.psum(stacked, 'box')]
    pallas_call x0 -> x1, Pallas kernels: none -> 108 us  [per_device(): pl.pallas_call(body, out_shape=jax.ShapeDtypeStruct((4, 16, 128), F32), i...]
    all_to_all x2 -> x0, waiting for transfers between devices: 42.6 us -> none  [apply_matrix(): lax.all_to_all(outgoing, 'box', split_axis=0, concat_axis=0, tiled=True)]
    gather x20 -> x0, local copies, waits for them, and re-layouts: 26.7 us -> none  [the longest x16 18.5 us: apply_classes(): received[jnp.maximum(picked, 0)]]
    dot_general x22 -> x0, matrix products: 26.6 us -> none  [the longest x16 24.5 us: apply_classes(): jnp.einsum('cqp,tcrp->trq', operators, sources, preferred_element_type=jn...]
    all_to_all x2 -> x0, starting transfers between devices: 22 us -> none  [apply_matrix(): lax.all_to_all(outgoing, 'box', split_axis=0, concat_axis=0, tiled=True)]
  transfers between devices with their start and end apart: 7 -> 0, of which waited for: 3 -> 0; matrix products, arithmetic and copies ran while one was open for 1% -> 0% of each run, Pallas kernels for 0% -> 0%
where the time goes in v2:
time: 116 us
  Pallas kernels  108 us (93%)
  local copies, waits for them, and re-layouts  4.74 us (4%)
  other arithmetic  2.3 us (2%)
    pallas_call x1, Pallas kernels, per_device(): pl.pallas_call(body, out_shape=jax.ShapeDtypeStruct((4, 16, 128), F32), i...  108 us
    eq x2, local copies, waits for them, and re-layouts, per_device(): table == jnp.arange(256, dtype=jnp.int32)  2.98 us

profile of v2, /device:TPU:1, one launch (start us, length us, event | category | flops | bytes accessed | tf_op | source)
XLA Modules:
  0.0 115.6 jit_solution(5448097186001010880)
XLA Ops:
  0.0 0.7 fusion.6
  0.7 1.0 select_reduce_fusion
  1.8 0.1 copy.16
  1.9 0.4 copy.21
  2.3 2.5 %eq.72 = s32[1024,2,256]{2,1,0:T(2,128)S(1)} broadcast(s32[1024,2]{1,0:T(8,128)S(1)} %bitcast.16), dimensions={0,1} | broadcast | bytes 2105344 | tf_op jit(solution)/shard_map/eq | solution.py:472
  4.9 0.2 copy.23
  5.0 0.0 copy-start.6
  5.1 0.0 copy-start.5
  5.1 0.0 copy-start
  5.1 0.0 copy-start.1
  5.1 0.0 copy-start.2
  5.1 0.0 copy-start.3
  5.1 0.0 copy-start.4
  5.2 0.3 compare_convert_fusion.oh_ref
  5.5 0.3 copy-done.6
  5.7 0.1 copy.20
  5.8 0.1 eq.82
  6.0 0.1 fusion.1.sendoh_ref
  6.1 0.0 copy-done.5
  6.1 0.1 copy.19
  6.2 0.1 eq.78
  6.3 0.1 fusion.nearoh_ref
  6.4 0.0 copy-done
  6.4 0.1 copy-done.1
  6.6 0.0 copy-done.2
  6.6 0.0 copy-done.3
  6.6 0.0 copy-done.4
  6.6 108.4 %shard_map.91 = f32[4,16,128]{2,1,0:T(8,128)S(1)} custom-call(f32[4,16,128]{2,1,0:T(8,128)S(1)} %copy-done.2, f32[16,128]{1,0:T(8,128)S(1)} %copy-done.4, bf16[16,256,128]{2,1,0:T(8,128)(2,1)S(1)} %copy-done, bf16[26,128,128]{2,1,0:T(8,128)(2,1)S(1)} %copy-done.1, bf16[64,256]{1,0:T(8,128)(2,1)S(1)} %bitcast.13, ...), custom_call_target="tpu_custom_call" | custom-call | flops 4000000000 | bytes 4000000 | tf_op jit(solution)/shard_map/pallas_call | solution.py:483
  115.0 0.6 copy.26
  (3 shorter events, 0.0 us)
Async XLA Ops:
  5.0 0.7 copy-start.6
  5.1 1.0 copy-start.5
  5.1 1.3 %copy-start = (bf16[16,256,128]{2,1,0:T(8,128)(2,1)S(1)}, bf16[16,256,128]{2,1,0:T(8,128)(2,1)}, u32[]{:S(2)}) copy-start(bf16[16,256,128]{2,1,0:T(8,128)(2,1)} %expand_hbm.1) | copy-start | bytes 3145732
  5.1 1.5 %copy-start.1 = (bf16[26,128,128]{2,1,0:T(8,128)(2,1)S(1)}, bf16[26,128,128]{2,1,0:T(8,128)(2,1)}, u32[]{:S(2)}) copy-start(bf16[26,128,128]{2,1,0:T(8,128)(2,1)} %near_hbm.1) | copy-start | bytes 2555908
  5.1 1.5 %copy-start.2 = (f32[4,16,128]{2,1,0:T(8,128)S(1)}, f32[4,16,128]{2,1,0:T(8,128)}, u32[]{:S(2)}) copy-start(f32[4,16,128]{2,1,0:T(8,128)} %rhs_ref.1) | copy-start | bytes 98308
  5.1 1.5 %copy-start.3 = (bf16[1,64,256]{2,1,0:T(8,128)(2,1)S(1)}, bf16[1,64,256]{2,1,0:T(8,128)(2,1)}, u32[]{:S(2)}) copy-start(bf16[1,64,256]{2,1,0:T(8,128)(2,1)} %param.13) | copy-start | bytes 98308
  5.1 1.4 %copy-start.4 = (f32[16,128]{1,0:T(8,128)S(1)}, f32[16,128]{1,0:T(8,128)}, u32[]{:S(2)}) copy-start(f32[16,128]{1,0:T(8,128)} %self_ref.1) | copy-start | bytes 24580

commit v3 on v2

v3 whole, which is shorter than its diff:
```python
import jax
import jax.numpy as jnp
from jax import lax
from jax.experimental import pallas as pl
from jax.experimental.pallas import tpu as pltpu
from jax.sharding import PartitionSpec as P

NZ, NY, NC, NX = 16, 4, 2, 4
NYC = NY * NC
SHIFT = 3.0
RADIUS = 3
NBOX_DEV = NZ * NYC
F32, BF16 = jnp.float32, jnp.bfloat16


def dot(a, b):
    return jnp.dot(a, b, preferred_element_type=F32)


def dot_nt(a, b):
    return lax.dot_general(a, b, (((1,), (1,)), ((), ())), preferred_element_type=F32)


def iota(shape, dim):
    return lax.broadcasted_iota(jnp.int32, shape, dim)


def peer_offsets():
    offsets = [
        (dz, dy, dc) for dz in range(NZ) for dy in range(NY) for dc in range(NC)
        if (dz, dy, dc) != (0, 0, 0)
    ]
    return sorted(offsets, key=lambda o: -(2 * min(o[0], NZ - o[0]) + 2 * min(o[1], NY - o[1]) + o[2]))


def body(
    rhs_hbm, self_hbm, expand_hbm, near_hbm, cls_hbm, near_src_hbm, rows_hbm, slot_hbm, class_hbm,
    out_ref,
    rhs_ref, self_ref, cls_ref, near_src_ref, rows_ref, slot_ref, class_ref,
    efull, nops, tout, tin, wbuf, hbuf, obuf, rbuf, r2, g2, nbuf, xbuf, tab, oh, nearoh, sendoh,
    rz_out, rz, ry_out, ry, ra_out, rall,
    load_sem, t_send, t_recv, ring_send, ring_recv, y_send, y_recv, sib_send, sib_recv,
    h_send, h_recv, a_send, a_recv, x_send, x_recv,
    rz_send, rz_recv, ry_send, ry_recv, ra_send, ra_recv,
):
    me = lax.axis_index("box")
    x = lax.axis_index("level")
    z = me // NYC
    yc = me % NYC
    y = yc // NC
    core = yc % NC
    sends = []
    mesh_ids = pl.DeviceIdType.MESH

    def remote(src, dst, ssem, rsem, box, level):
        return pltpu.make_async_remote_copy(
            src_ref=src, dst_ref=dst, send_sem=ssem, recv_sem=rsem,
            device_id=(box, level), device_id_type=mesh_ids,
        )

    def start(src, dst, ssem, rsem, box, level):
        copy = remote(src, dst, ssem, rsem, box, level)
        copy.start()
        sends.append(copy)

    def arrived(dst, rsem):
        remote(dst, dst, rsem, rsem, me, x).wait_recv()

    def sent(ref, ssem):
        remote(ref, ref, ssem, ssem, me, x).wait_send()

    def settle():
        for copy in sends:
            copy.wait_send()
        sends.clear()

    def box_at(offset):
        dz, dy, dc = offset
        return ((z + dz) % NZ) * NYC + ((y + dy) % NY) * NC + (core + dc) % NC

    def z_peer(d):
        return ((z + d) % NZ) * NYC + yc

    def p_peer(d):
        return z * NYC + (yc + d) % NYC

    def x_peer(d):
        return (x + d) % NX

    has_low = me > 0
    has_high = me < NBOX_DEV - 1

    barrier = pltpu.get_barrier_semaphore()
    offsets = peer_offsets()
    for offset in offsets:
        pl.semaphore_signal(barrier, inc=1, device_id=(box_at(offset), x), device_id_type=mesh_ids)
    for d in range(1, NX):
        pl.semaphore_signal(barrier, inc=1, device_id=(me, x_peer(d)), device_id_type=mesh_ids)

    loads = [
        pltpu.make_async_copy(src, dst, load_sem.at[i])
        for i, (src, dst) in enumerate((
            (cls_hbm, cls_ref), (rows_hbm, rows_ref), (rhs_hbm, rhs_ref), (expand_hbm, efull),
            (self_hbm, self_ref), (slot_hbm, slot_ref), (class_hbm, class_ref),
            (near_src_hbm, near_src_ref), (near_hbm, nops),
        ))
    ]
    for load in loads:
        load.start()
    loads[0].wait()

    eye2 = jnp.where(iota((64, 128), 0) == iota((64, 128), 1) % 64, 1.0, 0.0).astype(BF16)
    turned = lax.dot_general(
        cls_ref[...], eye2, (((0,), (0,)), ((), ())), preferred_element_type=F32
    ).astype(BF16)
    tout[...] = turned.reshape(NX, 64, 128)
    tin[x] = tout[x]

    loads[1].wait()
    for j in range(2):
        hot = jnp.where(iota((128, 128), 0) == rows_ref[j:j + 1, :], 1.0, 0.0)
        tab[pl.ds(j, 128, stride=2), :] = hot.T
    sendoh[...] = tab[0:256, :].astype(BF16)

    lane128 = iota((16, 128), 1)
    low16 = lane128 < 64
    row_t = iota((16, 128), 0)
    rows64 = iota((64, 256), 0) % 16

    def halo_fill(it, v):
        half = v.astype(BF16)
        for r in range(4):
            hbuf[it, 1, :, r * 128:(r + 1) * 128] = half[r * 16:(r + 1) * 16]
        return half

    def halo_sends(it):
        low = remote(hbuf.at[it, 1], hbuf.at[it, 2], h_send.at[it, 0], h_recv.at[it, 1], me - 1, x)
        high = remote(hbuf.at[it, 1], hbuf.at[it, 0], h_send.at[it, 1], h_recv.at[it, 0], me + 1, x)

        @pl.when(has_low)
        def _():
            low.start()

        @pl.when(has_high)
        def _():
            high.start()

        @pl.when(jnp.logical_not(has_low))
        def _():
            hbuf[it, 0] = jnp.zeros((16, 512), BF16)

        @pl.when(jnp.logical_not(has_high))
        def _():
            hbuf[it, 2] = jnp.zeros((16, 512), BF16)

        return low, high

    def halo_settle(low, high):
        @pl.when(has_low)
        def _():
            low.wait_send()

        @pl.when(has_high)
        def _():
            high.wait_send()

    def multipoles(it, half):
        band = efull[:, pl.ds(pl.multiple_of(x * 64, 64), 64), :].reshape(1024, 128)
        full = dot_nt(half, band)
        doubled = []
        for r in range(4):
            total = jnp.zeros((16, 128), F32)
            for j in range(8):
                piece = full[r * 16:(r + 1) * 16, j * 128:(j + 1) * 128]
                total = total + jnp.where(
                    row_t == 2 * j + jnp.where(low16, 0, 1), piece, 0.0
                )
            doubled.append(total + pltpu.roll(total, 64, 1))
        for h in range(2):
            rows = jnp.where(low16, doubled[2 * h], doubled[2 * h + 1]).astype(BF16)
            picked = dot(sendoh[:, 0:16], rows)
            obuf[it, h] = picked.astype(BF16).reshape(NBOX_DEV, 2, 128)

    def multipole_sends(it):
        for offset in offsets:
            to = box_at(offset)
            remote(obuf.at[it, :, to], rbuf.at[it, :, me], a_send.at[it], a_recv.at[it],
                   to, x).start()
        rbuf[it, :, me] = obuf[it, :, me]

    def many(it):
        return rbuf.at[it, :, pl.ds(0, NBOX_DEV - 1)]

    def near_field(it, low, high):
        @pl.when(has_low)
        def _():
            high.wait_recv()

        @pl.when(has_high)
        def _():
            low.wait_recv()

        nbuf[...] = dot(nearoh[...], hbuf[it].reshape(48, 512)).astype(BF16)

        def one(c, acc):
            rows = nbuf[pl.ds(pl.multiple_of(c * 16, 16), 16), :]
            lhs = jnp.concatenate([rows[:, r * 128:(r + 1) * 128] for r in range(4)], axis=0)
            return acc + dot_nt(lhs, nops[c])

        return lax.fori_loop(0, 26, one, jnp.zeros((64, 128), F32), unroll=2)

    def pick_sources(it):
        arrived(many(it), a_recv.at[it])
        low = iota((256, 128), 1) < 64
        for h in range(2):
            a = rbuf[it, h].reshape(256, 128).astype(F32)
            b = pltpu.roll(a, 64, 1)
            for r, first, second in ((2 * h, a, b), (2 * h + 1, b, a)):
                lanes = slice(r * 128, (r + 1) * 128)
                r2[0:256, lanes] = jnp.where(low, first, 0.0).astype(BF16)
                r2[256:512, lanes] = jnp.where(low, 0.0, second).astype(BF16)

        for i in range(4):
            picked = dot(oh[i * 256:(i + 1) * 256, :], r2[...]).astype(BF16)
            for k in range(16):
                for r in range(4):
                    g2[r * 16:(r + 1) * 16, (i * 16 + k) * 128:(i * 16 + k + 1) * 128] = (
                        picked[k * 16:(k + 1) * 16, r * 128:(r + 1) * 128]
                    )

    def local_far_sends(it):
        local = dot(g2[...], wbuf[...].reshape(8192, 256))
        far = jnp.zeros((64, 128), F32)
        for t in range(16):
            far = far + dot(jnp.where(rows64 == t, local, 0.0).astype(BF16), efull[t])
        xbuf[it, x] = far.astype(BF16)
        for d in (2, 1, 3):
            start(xbuf.at[it, x], xbuf.at[it, x], x_send.at[it, d], x_recv.at[it, x],
                  me, x_peer(d))

    def far_sum(it):
        for d in range(1, NX):
            arrived(xbuf.at[it, x_peer(d)], x_recv.at[it, x_peer(d)])
        total = xbuf[it, 0].astype(F32)
        for k in range(1, NX):
            total = total + xbuf[it, k].astype(F32)
        return total

    lane1 = iota((1, 128), 1)

    def packed(pairs):
        rows = []
        for a, b in pairs:
            product = a * b
            for r in range(4):
                rows.append(jnp.sum(product[r * 16:(r + 1) * 16], axis=0, keepdims=True))
        stacked = jnp.concatenate(rows, axis=0)
        sums = jnp.sum(stacked, axis=1, keepdims=True)
        shape = (len(rows), 128)
        return jnp.sum(
            jnp.where(iota(shape, 0) == iota(shape, 1), sums, 0.0), axis=0, keepdims=True
        )

    def reduce_z(row):
        rz_out[...] = row
        for d in range(1, NZ):
            start(rz_out, rz.at[z], rz_send.at[d], rz_recv.at[z], z_peer(d), x)
        rz[z] = row

    def reduce_p():
        for d in range(1, NZ):
            src = (z + d) % NZ
            arrived(rz.at[src], rz_recv.at[src])
        row = jnp.sum(rz[...], axis=0)
        ry_out[...] = row
        for d in range(1, NYC):
            start(ry_out, ry.at[yc], ry_send.at[d], ry_recv.at[yc], p_peer(d), x)
        ry[yc] = row

    def reduced():
        for d in range(1, NYC):
            src = (yc + d) % NYC
            arrived(ry.at[src], ry_recv.at[src])
        return jnp.sum(ry[...], axis=0)

    def reduce_all(row):
        ra_out[...] = row
        for offset in offsets:
            remote(ra_out, rall.at[me], ra_send, ra_recv, box_at(offset), x).start()
        rall[me] = row
        arrived(rall.at[pl.ds(0, NBOX_DEV - 1)], ra_recv)
        return jnp.sum(rall[...], axis=0)

    def spread(row):
        return jnp.concatenate(
            [
                jnp.broadcast_to(
                    jnp.sum(jnp.where(lane1 == r, row, 0.0), axis=1, keepdims=True), (16, 128)
                )
                for r in range(4)
            ],
            axis=0,
        )

    loads[2].wait()
    loads[4].wait()
    v = rhs_ref[...].reshape(64, 128)
    diag = jnp.concatenate([self_ref[...]] * 4, axis=0)
    half = halo_fill(0, v)
    loads[3].wait()
    multipoles(0, half)

    pl.semaphore_wait(barrier, NBOX_DEV - 1 + NX - 1)

    for d in (2, 1, 3):
        start(tout.at[x_peer(d)], tin.at[x], t_send.at[d], t_recv.at[x], me, x_peer(d))
    low_copy, high_copy = halo_sends(0)
    multipole_sends(0)

    iota_c = iota((128, 64), 0)
    for load in loads[5:8]:
        load.wait()
    for t in range(16):
        match = iota_c == class_ref[t:t + 1, :]
        value = jnp.where(match, (slot_ref[t:t + 1, :] + 1).astype(F32), 0.0)
        tab[pl.ds(t, 128, stride=16), :] = jnp.broadcast_to(
            jnp.sum(value, axis=1, keepdims=True), (128, 128)
        )

    for d in range(1, NX):
        arrived(tin.at[x_peer(d)], t_recv.at[x_peer(d)])
    low_t = iota((64, 128), 1) < 64
    merged = [
        jnp.where(low_t, tin[2 * h].astype(F32), tin[2 * h + 1].astype(F32)) for h in range(2)
    ]
    wbuf[me] = jnp.concatenate(merged, axis=1).astype(BF16)

    def cls_at(m, y_rel):
        return wbuf.at[((z - m + NZ) % NZ) * NYC + ((y + y_rel) % NY) * NC + core]

    def relay(m, reach):
        ref = cls_at(m, 0)
        ways = ((0, 1), (1, -1)) if m == 0 else (((0, 1),) if m <= NZ // 2 else ((1, -1),))
        gone = m if m <= NZ // 2 else NZ - m
        for d in range(RADIUS, 0, -1):
            for way, sign in ways:
                at = gone + d
                if at <= reach[way]:
                    start(ref, ref, ring_send.at[way, at], ring_recv.at[way, at],
                          z_peer(sign * d % NZ), x)

    reach = (NZ // 2, NZ // 2 - 1)

    def y_out(m):
        ref = cls_at(m, 0)
        up = z * NYC + ((y + 1) % NY) * NC + core
        down = z * NYC + ((y + 3) % NY) * NC + core
        start(ref, ref, y_send.at[0, m], y_recv.at[0, m], up, x)
        start(ref, ref, y_send.at[1, m], y_recv.at[1, m], down, x)

    def sibling(m, y_rel):
        ref = cls_at(m, y_rel)
        start(ref, ref, sib_send.at[y_rel, m], sib_recv, z * NYC + y * NC + 1 - core, x)

    def z_in(m):
        gone = m if m <= NZ // 2 else NZ - m
        way = 0 if m <= NZ // 2 else 1
        arrived(cls_at(m, 0), ring_recv.at[way, gone])
        if gone % RADIUS == 0:
            relay(m, reach)
        y_out(m)
        sibling(m, 0)

    def y_in(m):
        arrived(cls_at(m, 3), y_recv.at[0, m])
        arrived(cls_at(m, 1), y_recv.at[1, m])
        if m % 2 == 0:
            ref = cls_at(m, 3)
            to = z * NYC + ((y + 1) % NY) * NC + core
        else:
            ref = cls_at(m, 1)
            to = z * NYC + ((y + 3) % NY) * NC + core
        start(ref, ref, y_send.at[2, m], y_recv.at[2, m], to, x)
        sibling(m, 3)
        sibling(m, 1)

    def y_far_in(m):
        arrived(cls_at(m, 2), y_recv.at[2, m])
        sibling(m, 2)

    relay(0, reach)
    y_out(0)
    sibling(0, 0)

    def hot_rows(i, carry):
        at = pl.multiple_of(i * 32, 32)
        for k in range(2):
            want = tab[pl.ds(at + k * 16, 16), :]
            for part in range(2):
                slots = (lane128 + (part * 128 + 1)).astype(F32)
                oh[pl.ds(pl.multiple_of(i * 16, 16), 16),
                   k * 256 + part * 128:k * 256 + (part + 1) * 128] = jnp.where(
                       want == slots, 1.0, 0.0).astype(BF16)
        return carry

    lax.fori_loop(0, 64, hot_rows, 0, unroll=4)
    for c in range(26):
        nearoh[c * 16:(c + 1) * 16, :] = jnp.where(
            near_src_ref[:, c:c + 1] == iota((16, 48), 1), 1.0, 0.0
        ).astype(BF16)

    loads[8].wait()
    near_one = near_field(0, low_copy, high_copy)

    for m in (3, 13, 1, 15, 2, 14):
        z_in(m)
    y_in(0)
    for m in (6, 10):
        z_in(m)
    for m in (3, 13):
        y_in(m)
    for m in (4, 12, 5, 11):
        z_in(m)
    for m in (1, 15, 2, 14):
        y_in(m)
    y_far_in(0)
    for m in (8, 7, 9):
        z_in(m)
    pick_sources(0)
    for m in (6, 10, 4, 12, 5, 11):
        y_in(m)
    for m in (3, 13, 1, 15, 2, 14):
        y_far_in(m)
    for m in (8, 7, 9):
        y_in(m)
    for m in (6, 10, 4, 12, 5, 11, 8, 7, 9):
        y_far_in(m)
    arrived(wbuf.at[pl.ds(0, NBOX_DEV // 2)], sib_recv)

    local_far_sends(0)
    base = diag * v + near_one
    image = base + far_sum(0)

    shifted = image - SHIFT * v
    half = halo_fill(1, shifted)
    multipoles(1, half)
    multipole_sends(1)
    low_two, high_two = halo_sends(1)
    reduce_z(packed([(v, v), (v, image)]))
    near_two = near_field(1, low_two, high_two)
    sent(many(0), a_send.at[0])
    halo_settle(low_copy, high_copy)
    reduce_p()
    pick_sources(1)
    local_far_sends(1)

    rr = reduced()
    ra = pltpu.roll(rr, 124, 1)
    h11 = ra / rr
    slope = spread(h11)
    u = image - slope * v
    base = diag * shifted + near_two - (slope - SHIFT) * image
    settle()
    halo_settle(low_two, high_two)
    sent(many(1), a_send.at[1])
    b = base + far_sum(1)
    uu = reduce_all(packed([(u, u), (v, b), (u, b), (b, b)]))
    rb = pltpu.roll(uu, 124, 1)
    ub = pltpu.roll(uu, 120, 1)
    bb = pltpu.roll(uu, 116, 1)
    beta = jnp.sqrt(rr)
    length = jnp.sqrt(uu)
    h21 = length / beta
    h12 = rb / (beta * length)
    h22 = ub / uu
    gram_aa = h11 * h11 + h21 * h21
    gram_ab = h11 * h12 + h21 * h22
    gram_bb = bb / uu
    right_a = beta * h11
    right_b = beta * h12
    det = gram_aa * gram_bb - gram_ab * gram_ab
    coef_a = (gram_bb * right_a - gram_ab * right_b) / det / beta
    coef_b = (gram_aa * right_b - gram_ab * right_a) / det / length
    out_ref[...] = (spread(coef_a) * v + spread(coef_b) * u).reshape(4, 16, 128)
    sent(rall.at[pl.ds(0, NBOX_DEV - 1)], ra_send)


def per_device(
    rhs_field, self_coef, expand, near_ops, class_ops, near_src, send_rows, list_slot, list_class
):
    vmem = pl.BlockSpec(memory_space=pltpu.VMEM)
    hbm = pl.BlockSpec(memory_space=pltpu.HBM)
    dma = pltpu.SemaphoreType.DMA
    return pl.pallas_call(
        body,
        out_shape=jax.ShapeDtypeStruct((4, 16, 128), F32),
        in_specs=[hbm] * 9,
        out_specs=vmem,
        scratch_shapes=[
            pltpu.VMEM((4, 16, 128), F32),
            pltpu.VMEM((16, 128), F32),
            pltpu.VMEM((64, 256), BF16),
            pltpu.VMEM((16, 26), jnp.int32),
            pltpu.VMEM((2, 128), jnp.int32),
            pltpu.VMEM((16, 64), jnp.int32),
            pltpu.VMEM((16, 64), jnp.int32),
            pltpu.VMEM((16, 256, 128), BF16),
            pltpu.VMEM((26, 128, 128), BF16),
            pltpu.VMEM((NX, 64, 128), BF16),
            pltpu.VMEM((NX, 64, 128), BF16),
            pltpu.VMEM((NBOX_DEV, 64, 256), BF16),
            pltpu.VMEM((2, 3, 16, 512), BF16),
            pltpu.VMEM((2, 2, NBOX_DEV, 2, 128), BF16),
            pltpu.VMEM((2, 2, NBOX_DEV, 2, 128), BF16),
            pltpu.VMEM((512, 512), BF16),
            pltpu.VMEM((64, 8192), BF16),
            pltpu.VMEM((416, 512), BF16),
            pltpu.VMEM((2, NX, 64, 128), BF16),
            pltpu.VMEM((2048, 128), F32),
            pltpu.VMEM((1024, 512), BF16),
            pltpu.VMEM((416, 48), BF16),
            pltpu.VMEM((256, 128), BF16),
            pltpu.VMEM((1, 128), F32),
            pltpu.VMEM((NZ, 1, 128), F32),
            pltpu.VMEM((1, 128), F32),
            pltpu.VMEM((NYC, 1, 128), F32),
            pltpu.VMEM((1, 128), F32),
            pltpu.VMEM((NBOX_DEV, 1, 128), F32),
            dma((9,)),
            dma((NX,)), dma((NX,)),
            dma((2, 9)), dma((2, 9)),
            dma((3, NZ)), dma((3, NZ)),
            dma((NY, NZ)), dma,
            dma((2, 2)), dma((2, 2)),
            dma((2,)), dma((2,)),
            dma((2, NX)), dma((2, NX)),
            dma((NZ,)), dma((NZ,)),
            dma((NYC,)), dma((NYC,)),
            dma, dma,
        ],
        compiler_params=pltpu.CompilerParams(
            collective_id=0, has_side_effects=True, vmem_limit_bytes=62 * 1024 * 1024
        ),
        cost_estimate=pl.CostEstimate(
            flops=4_000_000_000, bytes_accessed=4_000_000, transcendentals=0
        ),
    )(
        rhs_field, self_coef, expand, near_ops, class_ops[0], near_src, send_rows[0].T,
        list_slot, list_class,
    )


def solution(mesh):
    return jax.shard_map(
        per_device,
        mesh=mesh,
        in_specs=(
            P(None, "box", None),
            P("box", None),
            P("box", None, None),
            P(),
            P("box", "level", None),
            P("box", None),
            P("box", None, None),
            P("box", None),
            P("box", None),
        ),
        out_specs=P(None, "box", None),
        check_vma=False,
    )
```

time: 116 us -> 86.4 us (0.74)
  Pallas kernels: 108 us -> 84.8 us
  local copies, waits for them, and re-layouts: 4.74 us -> 1.38 us
  other arithmetic: 2.3 us -> 0 us
    pallas_call x1, Pallas kernels: 108 us -> 84.8 us  [per_device(): pl.pallas_call(body, out_shape=jax.ShapeDtypeStruct((4, 16, 128), F32), i...]
    eq x4 -> x0, local copies, waits for them, and re-layouts: 3.19 us -> none  [the longest x2 2.98 us: per_device(): table == jnp.arange(256, dtype=jnp.int32)]
where the time goes in v3:
time: 86.4 us; the launch traced here: 86.2 us
  Pallas kernels  84.8 us (98%)
  local copies, waits for them, and re-layouts  1.38 us (2%)
    pallas_call x1, Pallas kernels, per_device(): pl.pallas_call(body, out_shape=jax.ShapeDtypeStruct((4, 16, 128), F32), i...  84.8 us

profile of v3, /device:TPU:1, one launch (start us, length us, event | category | flops | bytes accessed | tf_op | source)
XLA Modules:
  0.0 86.2 jit_solution(13353697196414401206)
XLA Ops:
  0.0 84.8 %shard_map.91 = f32[4,16,128]{2,1,0:T(8,128)} custom-call(f32[4,16,128]{2,1,0:T(8,128)} %rhs_hbm.1, f32[16,128]{1,0:T(8,128)} %self_hbm.1, bf16[16,256,128]{2,1,0:T(8,128)(2,1)} %expand_hbm.1, bf16[26,128,128]{2,1,0:T(8,128)(2,1)} %near_hbm.1, bf16[64,256]{1,0:T(8,128)(2,1)} %bitcast.4, s32[16,26]{1,0:T(8,128)} %near_src_hbm.1, s32[2,128]{1,0:T(2,128)} %bitcast.5, ...), custom_call_target="tpu_custom_call" | custom-call | flops 4000000000 | bytes 4000000 | tf_op jit(solution)/shard_map/pallas_call | solution.py:494
  84.8 1.4 %copy.11 = f32[4,16,128]{2,1,0:T(8,128)} copy(f32[4,16,128]{2,1,0:T(8,128)} %shard_map.91) | data formatting | bytes 65536

commit v4 on v3

--- a/solution.py
+++ b/solution.py
@@ -9,6 +9,10 @@
 NYC = NY * NC
 SHIFT = 3.0
 RADIUS = 3
+HOP = 2
+FAR_DIRECT = (7, 8, 9)
+EARLY = (0, 1, 15, 2, 14, 3, 13, 4, 12)
+LATE = (5, 11, 6, 10, 7, 9, 8)
 NBOX_DEV = NZ * NYC
 F32, BF16 = jnp.float32, jnp.bfloat16
 
@@ -41,7 +45,7 @@
     rz_out, rz, ry_out, ry, ra_out, rall,
     load_sem, t_send, t_recv, ring_send, ring_recv, y_send, y_recv, sib_send, sib_recv,
     h_send, h_recv, a_send, a_recv, x_send, x_recv,
-    rz_send, rz_recv, ry_send, ry_recv, ra_send, ra_recv,
+    rz_send, rz_recv, ry_send, ry_recv, ra_send, ra_recv, known,
 ):
     me = lax.axis_index("box")
     x = lax.axis_index("level")
@@ -92,10 +96,17 @@
 
     barrier = pltpu.get_barrier_semaphore()
     offsets = peer_offsets()
-    for offset in offsets:
-        pl.semaphore_signal(barrier, inc=1, device_id=(box_at(offset), x), device_id_type=mesh_ids)
-    for d in range(1, NX):
-        pl.semaphore_signal(barrier, inc=1, device_id=(me, x_peer(d)), device_id_type=mesh_ids)
+
+    def signal(sem, box, level):
+        pl.semaphore_signal(sem, inc=1, device_id=(box, level), device_id_type=mesh_ids)
+
+    near_z = [d % NZ for k in range(RADIUS, 0, -1) for d in (k, -k)]
+    for d in (2, 1, 3):
+        signal(barrier, me, x_peer(d))
+    for d in near_z:
+        signal(barrier, z_peer(d), x)
+    for d in range(1, NYC):
+        signal(barrier, p_peer(d), x)
 
     loads = [
         pltpu.make_async_copy(src, dst, load_sem.at[i])
@@ -115,6 +126,26 @@
     ).astype(BF16)
     tout[...] = turned.reshape(NX, 64, 128)
     tin[x] = tout[x]
+
+    pl.semaphore_wait(barrier, NX - 1 + len(near_z) + NYC - 1)
+    for d in (2, 1, 3):
+        start(tout.at[x_peer(d)], tin.at[x], t_send.at[d], t_recv.at[x], me, x_peer(d))
+
+    for d in near_z:
+        signal(known.at[0], z_peer(d), x)
+
+    def know_two():
+        pl.semaphore_wait(known.at[0], len(near_z))
+        for d in (RADIUS, NZ - RADIUS):
+            signal(known.at[1], z_peer(d), x)
+
+    def know_three():
+        pl.semaphore_wait(known.at[1], 2)
+        for d in (NZ // 2 - 2 * RADIUS, NZ // 2 + 2 * RADIUS):
+            signal(known.at[2], z_peer(d), x)
+
+    def know_all():
+        pl.semaphore_wait(known.at[2], 2)
 
     loads[1].wait()
     for j in range(2):
@@ -181,12 +212,15 @@
             picked = dot(sendoh[:, 0:16], rows)
             obuf[it, h] = picked.astype(BF16).reshape(NBOX_DEV, 2, 128)
 
-    def multipole_sends(it):
+    def multipole_sends(it, least=0, most=NZ):
         for offset in offsets:
+            if not least <= min(offset[0], NZ - offset[0]) <= most:
+                continue
             to = box_at(offset)
             remote(obuf.at[it, :, to], rbuf.at[it, :, me], a_send.at[it], a_recv.at[it],
                    to, x).start()
-        rbuf[it, :, me] = obuf[it, :, me]
+        if least == 0:
+            rbuf[it, :, me] = obuf[it, :, me]
 
     def many(it):
         return rbuf.at[it, :, pl.ds(0, NBOX_DEV - 1)]
@@ -228,8 +262,16 @@
                         picked[k * 16:(k + 1) * 16, r * 128:(r + 1) * 128]
                     )
 
-    def local_far_sends(it):
-        local = dot(g2[...], wbuf[...].reshape(8192, 256))
+    def planes_product(group, part):
+        arrived(wbuf.at[pl.ds(0, len(group) * NY)], sib_recv.at[part])
+        total = jnp.zeros((64, 256), F32)
+        for m in group:
+            plane = (z - m + NZ) % NZ
+            rows = g2[:, pl.ds(pl.multiple_of(plane * 512, 512), 512)]
+            total = total + dot(rows, wbuf[pl.ds(plane * NYC, NYC)].reshape(512, 256))
+        return total
+
+    def local_far_sends(it, local):
         far = jnp.zeros((64, 128), F32)
         for t in range(16):
             far = far + dot(jnp.where(rows64 == t, local, 0.0).astype(BF16), efull[t])
@@ -310,12 +352,75 @@
     loads[3].wait()
     multipoles(0, half)
 
-    pl.semaphore_wait(barrier, NBOX_DEV - 1 + NX - 1)
-
-    for d in (2, 1, 3):
-        start(tout.at[x_peer(d)], tin.at[x], t_send.at[d], t_recv.at[x], me, x_peer(d))
-    low_copy, high_copy = halo_sends(0)
-    multipole_sends(0)
+    for d in range(1, NX):
+        arrived(tin.at[x_peer(d)], t_recv.at[x_peer(d)])
+    low_t = iota((64, 128), 1) < 64
+    merged = [
+        jnp.where(low_t, tin[2 * h].astype(F32), tin[2 * h + 1].astype(F32)) for h in range(2)
+    ]
+    wbuf[me] = jnp.concatenate(merged, axis=1).astype(BF16)
+
+    def cls_at(m, y_rel):
+        return wbuf.at[((z - m + NZ) % NZ) * NYC + ((y + y_rel) % NY) * NC + core]
+
+    def relay(m, reach):
+        ref = cls_at(m, 0)
+        ways = ((0, 1), (1, -1)) if m == 0 else (((0, 1),) if m <= NZ // 2 else ((1, -1),))
+        gone = m if m <= NZ // 2 else NZ - m
+        for d in range(HOP, 0, -1):
+            for way, sign in ways:
+                at = gone + d
+                if at <= reach[way]:
+                    start(ref, ref, ring_send.at[way, at], ring_recv.at[way, at],
+                          z_peer(sign * d % NZ), x)
+
+    reach = (NZ // 2, NZ // 2 - 1)
+
+    def y_out(m):
+        ref = cls_at(m, 0)
+        up = z * NYC + ((y + 1) % NY) * NC + core
+        down = z * NYC + ((y + 3) % NY) * NC + core
+        start(ref, ref, y_send.at[0, m], y_recv.at[0, m], up, x)
+        start(ref, ref, y_send.at[1, m], y_recv.at[1, m], down, x)
+        if m in FAR_DIRECT:
+            across = z * NYC + ((y + 2) % NY) * NC + core
+            start(ref, ref, y_send.at[2, m], y_recv.at[2, m], across, x)
+
+    def sibling(m, y_rel):
+        ref = cls_at(m, y_rel)
+        start(ref, ref, sib_send.at[y_rel, m], sib_recv.at[0 if m in EARLY else 1],
+              z * NYC + y * NC + 1 - core, x)
+
+    def z_in(m):
+        gone = m if m <= NZ // 2 else NZ - m
+        way = 0 if m <= NZ // 2 else 1
+        arrived(cls_at(m, 0), ring_recv.at[way, gone])
+        if gone % HOP == 0:
+            relay(m, reach)
+        y_out(m)
+        sibling(m, 0)
+
+    def y_in(m):
+        arrived(cls_at(m, 3), y_recv.at[0, m])
+        arrived(cls_at(m, 1), y_recv.at[1, m])
+        if m not in FAR_DIRECT:
+            if m % 2 == 0:
+                ref = cls_at(m, 3)
+                to = z * NYC + ((y + 1) % NY) * NC + core
+            else:
+                ref = cls_at(m, 1)
+                to = z * NYC + ((y + 3) % NY) * NC + core
+            start(ref, ref, y_send.at[2, m], y_recv.at[2, m], to, x)
+        sibling(m, 3)
+        sibling(m, 1)
+
+    def y_far_in(m):
+        arrived(cls_at(m, 2), y_recv.at[2, m])
+        sibling(m, 2)
+
+    relay(0, reach)
+    y_out(0)
+    sibling(0, 0)
 
     iota_c = iota((128, 64), 0)
     for load in loads[5:8]:
@@ -326,71 +431,6 @@
         tab[pl.ds(t, 128, stride=16), :] = jnp.broadcast_to(
             jnp.sum(value, axis=1, keepdims=True), (128, 128)
         )
-
-    for d in range(1, NX):
-        arrived(tin.at[x_peer(d)], t_recv.at[x_peer(d)])
-    low_t = iota((64, 128), 1) < 64
-    merged = [
-        jnp.where(low_t, tin[2 * h].astype(F32), tin[2 * h + 1].astype(F32)) for h in range(2)
-    ]
-    wbuf[me] = jnp.concatenate(merged, axis=1).astype(BF16)
-
-    def cls_at(m, y_rel):
-        return wbuf.at[((z - m + NZ) % NZ) * NYC + ((y + y_rel) % NY) * NC + core]
-
-    def relay(m, reach):
-        ref = cls_at(m, 0)
-        ways = ((0, 1), (1, -1)) if m == 0 else (((0, 1),) if m <= NZ // 2 else ((1, -1),))
-        gone = m if m <= NZ // 2 else NZ - m
-        for d in range(RADIUS, 0, -1):
-            for way, sign in ways:
-                at = gone + d
-                if at <= reach[way]:
-                    start(ref, ref, ring_send.at[way, at], ring_recv.at[way, at],
-                          z_peer(sign * d % NZ), x)
-
-    reach = (NZ // 2, NZ // 2 - 1)
-
-    def y_out(m):
-        ref = cls_at(m, 0)
-        up = z * NYC + ((y + 1) % NY) * NC + core
-        down = z * NYC + ((y + 3) % NY) * NC + core
-        start(ref, ref, y_send.at[0, m], y_recv.at[0, m], up, x)
-        start(ref, ref, y_send.at[1, m], y_recv.at[1, m], down, x)
-
-    def sibling(m, y_rel):
-        ref = cls_at(m, y_rel)
-        start(ref, ref, sib_send.at[y_rel, m], sib_recv, z * NYC + y * NC + 1 - core, x)
-
-    def z_in(m):
-        gone = m if m <= NZ // 2 else NZ - m
-        way = 0 if m <= NZ // 2 else 1
-        arrived(cls_at(m, 0), ring_recv.at[way, gone])
-        if gone % RADIUS == 0:
-            relay(m, reach)
-        y_out(m)
-        sibling(m, 0)
-
-    def y_in(m):
-        arrived(cls_at(m, 3), y_recv.at[0, m])
-        arrived(cls_at(m, 1), y_recv.at[1, m])
-        if m % 2 == 0:
-            ref = cls_at(m, 3)
-            to = z * NYC + ((y + 1) % NY) * NC + core
-        else:
-            ref = cls_at(m, 1)
-            to = z * NYC + ((y + 3) % NY) * NC + core
-        start(ref, ref, y_send.at[2, m], y_recv.at[2, m], to, x)
-        sibling(m, 3)
-        sibling(m, 1)
-
-    def y_far_in(m):
-        arrived(cls_at(m, 2), y_recv.at[2, m])
-        sibling(m, 2)
-
-    relay(0, reach)
-    y_out(0)
-    sibling(0, 0)
 
     def hot_rows(i, carry):
         at = pl.multiple_of(i * 32, 32)
@@ -404,40 +444,49 @@
         return carry
 
     lax.fori_loop(0, 64, hot_rows, 0, unroll=4)
+    know_two()
+    low_copy, high_copy = halo_sends(0)
+    multipole_sends(0, 0, 3)
+    for m in (2, 14, 1, 15):
+        z_in(m)
+    y_in(0)
+    know_three()
+    multipole_sends(0, 4, 6)
     for c in range(26):
         nearoh[c * 16:(c + 1) * 16, :] = jnp.where(
             near_src_ref[:, c:c + 1] == iota((16, 48), 1), 1.0, 0.0
         ).astype(BF16)
 
     loads[8].wait()
+    for m in (4, 12, 3, 13):
+        z_in(m)
+    for m in (2, 14, 1, 15):
+        y_in(m)
+    know_all()
+    multipole_sends(0, 7, 8)
     near_one = near_field(0, low_copy, high_copy)
-
-    for m in (3, 13, 1, 15, 2, 14):
+    for m in (6, 10, 5, 11):
         z_in(m)
-    y_in(0)
-    for m in (6, 10):
-        z_in(m)
-    for m in (3, 13):
+    y_far_in(0)
+    for m in (4, 12, 3, 13):
         y_in(m)
-    for m in (4, 12, 5, 11):
-        z_in(m)
-    for m in (1, 15, 2, 14):
-        y_in(m)
-    y_far_in(0)
     for m in (8, 7, 9):
         z_in(m)
+    for m in (2, 14, 1, 15):
+        y_far_in(m)
+    for m in (6, 10, 5, 11):
+        y_in(m)
     pick_sources(0)
-    for m in (6, 10, 4, 12, 5, 11):
-        y_in(m)
-    for m in (3, 13, 1, 15, 2, 14):
+    for m in (4, 12, 3, 13):
         y_far_in(m)
     for m in (8, 7, 9):
         y_in(m)
-    for m in (6, 10, 4, 12, 5, 11, 8, 7, 9):
+    local_one = planes_product(EARLY, 0)
+    for m in (6, 10, 5, 11, 8, 7, 9):
         y_far_in(m)
-    arrived(wbuf.at[pl.ds(0, NBOX_DEV // 2)], sib_recv)
-
-    local_far_sends(0)
+    local_one = local_one + planes_product(LATE, 1)
+
+    local_far_sends(0, local_one)
     base = diag * v + near_one
     image = base + far_sum(0)
 
@@ -452,7 +501,7 @@
     halo_settle(low_copy, high_copy)
     reduce_p()
     pick_sources(1)
-    local_far_sends(1)
+    local_far_sends(1, dot(g2[...], wbuf[...].reshape(8192, 256)))
 
     rr = reduced()
     ra = pltpu.roll(rr, 124, 1)
@@ -530,13 +579,14 @@
             dma((NX,)), dma((NX,)),
             dma((2, 9)), dma((2, 9)),
             dma((3, NZ)), dma((3, NZ)),
-            dma((NY, NZ)), dma,
+            dma((NY, NZ)), dma((2,)),
             dma((2, 2)), dma((2, 2)),
             dma((2,)), dma((2,)),
             dma((2, NX)), dma((2, NX)),
             dma((NZ,)), dma((NZ,)),
             dma((NYC,)), dma((NYC,)),
             dma, dma,
+            pltpu.SemaphoreType.REGULAR((3,)),
         ],
         compiler_params=pltpu.CompilerParams(
             collective_id=0, has_side_effects=True, vmem_limit_bytes=62 * 1024 * 1024

time: 86.4 us -> 78.9 us (0.913)
  Pallas kernels: 84.8 us -> 77.4 us
    pallas_call x1, Pallas kernels: 84.8 us -> 77.4 us  [per_device(): pl.pallas_call(body, out_shape=jax.ShapeDtypeStruct((4, 16, 128), F32), i...]
where the time goes in v4:
time: 78.9 us; the launch traced here: 78.8 us
  Pallas kernels  77.4 us (98%)
  local copies, waits for them, and re-layouts  1.38 us (2%)
    pallas_call x1, Pallas kernels, per_device(): pl.pallas_call(body, out_shape=jax.ShapeDtypeStruct((4, 16, 128), F32), i...  77.4 us

profile of v4, /device:TPU:1, one launch (start us, length us, event | category | flops | bytes accessed | tf_op | source)
XLA Modules:
  0.0 78.8 jit_solution(2912664074310028848)
XLA Ops:
  0.0 77.4 %shard_map.91 = f32[4,16,128]{2,1,0:T(8,128)} custom-call(f32[4,16,128]{2,1,0:T(8,128)} %rhs_hbm.1, f32[16,128]{1,0:T(8,128)} %self_hbm.1, bf16[16,256,128]{2,1,0:T(8,128)(2,1)} %expand_hbm.1, bf16[26,128,128]{2,1,0:T(8,128)(2,1)} %near_hbm.1, bf16[64,256]{1,0:T(8,128)(2,1)} %bitcast.4, s32[16,26]{1,0:T(8,128)} %near_src_hbm.1, s32[2,128]{1,0:T(2,128)} %bitcast.5, ...), custom_call_target="tpu_custom_call" | custom-call | flops 4000000000 | bytes 4000000 | tf_op jit(solution)/shard_map/pallas_call | solution.py:543
  77.4 1.4 %copy.11 = f32[4,16,128]{2,1,0:T(8,128)} copy(f32[4,16,128]{2,1,0:T(8,128)} %shard_map.91) | data formatting | bytes 65536

commit v5 on v4

--- a/solution.py
+++ b/solution.py
@@ -67,6 +67,12 @@
         copy.start()
         sends.append(copy)
 
+    blocks = {"ring": 0, "y": 0, "sib": 0}
+
+    def pass_on(kind, ref, ssem, rsem, box):
+        remote(ref, ref, ssem, rsem, box, x).start()
+        blocks[kind] += 1
+
     def arrived(dst, rsem):
         remote(dst, dst, rsem, rsem, me, x).wait_recv()
 
@@ -306,23 +312,19 @@
     def reduce_z(row):
         rz_out[...] = row
         for d in range(1, NZ):
-            start(rz_out, rz.at[z], rz_send.at[d], rz_recv.at[z], z_peer(d), x)
+            remote(rz_out, rz.at[z], rz_send, rz_recv, z_peer(d), x).start()
         rz[z] = row
 
     def reduce_p():
-        for d in range(1, NZ):
-            src = (z + d) % NZ
-            arrived(rz.at[src], rz_recv.at[src])
+        arrived(rz.at[pl.ds(0, NZ - 1)], rz_recv)
         row = jnp.sum(rz[...], axis=0)
         ry_out[...] = row
         for d in range(1, NYC):
-            start(ry_out, ry.at[yc], ry_send.at[d], ry_recv.at[yc], p_peer(d), x)
+            remote(ry_out, ry.at[yc], ry_send, ry_recv, p_peer(d), x).start()
         ry[yc] = row
 
     def reduced():
-        for d in range(1, NYC):
-            src = (yc + d) % NYC
-            arrived(ry.at[src], ry_recv.at[src])
+        arrived(ry.at[pl.ds(0, NYC - 1)], ry_recv)
         return jnp.sum(ry[...], axis=0)
 
     def reduce_all(row):
@@ -371,8 +373,8 @@
             for way, sign in ways:
                 at = gone + d
                 if at <= reach[way]:
-                    start(ref, ref, ring_send.at[way, at], ring_recv.at[way, at],
-                          z_peer(sign * d % NZ), x)
+                    pass_on("ring", ref, ring_send, ring_recv.at[way, at],
+                            z_peer(sign * d % NZ))
 
     reach = (NZ // 2, NZ // 2 - 1)
 
@@ -380,16 +382,16 @@
         ref = cls_at(m, 0)
         up = z * NYC + ((y + 1) % NY) * NC + core
         down = z * NYC + ((y + 3) % NY) * NC + core
-        start(ref, ref, y_send.at[0, m], y_recv.at[0, m], up, x)
-        start(ref, ref, y_send.at[1, m], y_recv.at[1, m], down, x)
+        pass_on("y", ref, y_send, y_recv.at[0, m], up)
+        pass_on("y", ref, y_send, y_recv.at[1, m], down)
         if m in FAR_DIRECT:
             across = z * NYC + ((y + 2) % NY) * NC + core
-            start(ref, ref, y_send.at[2, m], y_recv.at[2, m], across, x)
+            pass_on("y", ref, y_send, y_recv.at[2, m], across)
 
     def sibling(m, y_rel):
         ref = cls_at(m, y_rel)
-        start(ref, ref, sib_send.at[y_rel, m], sib_recv.at[0 if m in EARLY else 1],
-              z * NYC + y * NC + 1 - core, x)
+        pass_on("sib", ref, sib_send, sib_recv.at[0 if m in EARLY else 1],
+                z * NYC + y * NC + 1 - core)
 
     def z_in(m):
         gone = m if m <= NZ // 2 else NZ - m
@@ -410,7 +412,7 @@
             else:
                 ref = cls_at(m, 1)
                 to = z * NYC + ((y + 3) % NY) * NC + core
-            start(ref, ref, y_send.at[2, m], y_recv.at[2, m], to, x)
+            pass_on("y", ref, y_send, y_recv.at[2, m], to)
         sibling(m, 3)
         sibling(m, 1)
 
@@ -492,15 +494,18 @@
 
     shifted = image - SHIFT * v
     half = halo_fill(1, shifted)
+    low_two, high_two = halo_sends(1)
     multipoles(1, half)
     multipole_sends(1)
-    low_two, high_two = halo_sends(1)
     reduce_z(packed([(v, v), (v, image)]))
     near_two = near_field(1, low_two, high_two)
     sent(many(0), a_send.at[0])
     halo_settle(low_copy, high_copy)
+    for kind, ssem in (("ring", ring_send), ("y", y_send), ("sib", sib_send)):
+        sent(wbuf.at[pl.ds(0, blocks[kind])], ssem)
+    settle()
+    pick_sources(1)
     reduce_p()
-    pick_sources(1)
     local_far_sends(1, dot(g2[...], wbuf[...].reshape(8192, 256)))
 
     rr = reduced()
@@ -509,9 +514,6 @@
     slope = spread(h11)
     u = image - slope * v
     base = diag * shifted + near_two - (slope - SHIFT) * image
-    settle()
-    halo_settle(low_two, high_two)
-    sent(many(1), a_send.at[1])
     b = base + far_sum(1)
     uu = reduce_all(packed([(u, u), (v, b), (u, b), (b, b)]))
     rb = pltpu.roll(uu, 124, 1)
@@ -531,6 +533,11 @@
     coef_a = (gram_bb * right_a - gram_ab * right_b) / det / beta
     coef_b = (gram_aa * right_b - gram_ab * right_a) / det / length
     out_ref[...] = (spread(coef_a) * v + spread(coef_b) * u).reshape(4, 16, 128)
+    settle()
+    halo_settle(low_two, high_two)
+    sent(many(1), a_send.at[1])
+    sent(rz.at[pl.ds(0, NZ - 1)], rz_send)
+    sent(ry.at[pl.ds(0, NYC - 1)], ry_send)
     sent(rall.at[pl.ds(0, NBOX_DEV - 1)], ra_send)
 
 
@@ -577,14 +584,14 @@
             pltpu.VMEM((NBOX_DEV, 1, 128), F32),
             dma((9,)),
             dma((NX,)), dma((NX,)),
-            dma((2, 9)), dma((2, 9)),
-            dma((3, NZ)), dma((3, NZ)),
-            dma((NY, NZ)), dma((2,)),
+            dma, dma((2, 9)),
+            dma, dma((3, NZ)),
+            dma, dma((2,)),
             dma((2, 2)), dma((2, 2)),
             dma((2,)), dma((2,)),
             dma((2, NX)), dma((2, NX)),
-            dma((NZ,)), dma((NZ,)),
-            dma((NYC,)), dma((NYC,)),
+            dma, dma,
+            dma, dma,
             dma, dma,
             pltpu.SemaphoreType.REGULAR((3,)),
         ],

time: 78.9 us -> 77.1 us (0.977)
  Pallas kernels: 77.4 us -> 75.5 us
    pallas_call x1, Pallas kernels: 77.4 us -> 75.5 us  [per_device(): pl.pallas_call(body, out_shape=jax.ShapeDtypeStruct((4, 16, 128), F32), i...]
where the time goes in v5:
time: 77.1 us; the launch traced here: 76.9 us
  Pallas kernels  75.5 us (98%)
  local copies, waits for them, and re-layouts  1.38 us (2%)
    pallas_call x1, Pallas kernels, per_device(): pl.pallas_call(body, out_shape=jax.ShapeDtypeStruct((4, 16, 128), F32), i...  75.5 us

profile of v5, /device:TPU:1, one launch (start us, length us, event | category | flops | bytes accessed | tf_op | source)
XLA Modules:
  0.0 76.9 jit_solution(8655859828028610182)
XLA Ops:
  0.0 75.5 %shard_map.91 = f32[4,16,128]{2,1,0:T(8,128)} custom-call(f32[4,16,128]{2,1,0:T(8,128)} %rhs_hbm.1, f32[16,128]{1,0:T(8,128)} %self_hbm.1, bf16[16,256,128]{2,1,0:T(8,128)(2,1)} %expand_hbm.1, bf16[26,128,128]{2,1,0:T(8,128)(2,1)} %near_hbm.1, bf16[64,256]{1,0:T(8,128)(2,1)} %bitcast.4, s32[16,26]{1,0:T(8,128)} %near_src_hbm.1, s32[2,128]{1,0:T(2,128)} %bitcast.5, ...), custom_call_target="tpu_custom_call" | custom-call | flops 4000000000 | bytes 4000000 | tf_op jit(solution)/shard_map/pallas_call | solution.py:550
  75.5 1.4 %copy.11 = f32[4,16,128]{2,1,0:T(8,128)} copy(f32[4,16,128]{2,1,0:T(8,128)} %shard_map.91) | data formatting | bytes 65536
